TPU v7x, 128 devices: a whole 4x4x4 slice. The times are simulated.
128 devices in a mesh: ctx: 16 (over x, y_hi, core), tp: 8 (over y_lo, z).
Axes of the slice: x: 4, y: 4 (y_hi: 2, y_lo: 2; y = y_hi * 2 + y_lo), z: 4, core: 2. Of those that a mesh axis runs over, the one named last changes fastest.
Arguments:
- queries: bfloat16 [4096, 8192], P('ctx', 'tp'), may hold values from -120 to 120
- key_proj: bfloat16 [4096, 1024], P('ctx', 'tp'), may hold values from -4 to 4
- value_proj: bfloat16 [4096, 1024], P('ctx', 'tp'), may hold values from -6 to 6
- out_weight: bfloat16 [8192, 8192], P('tp'), may hold values from -0.75 to 0.75
- doc_ids: int32 [4096], replicated, may hold values from 0 to 7, never falling along the last dimension, each value on 1 to 2048 neighbouring positions
- drop_seed: int32 [1], replicated, may hold values from 0 to 1073741823
Outputs:
- output: bfloat16 [4096, 8192], P('ctx', 'tp')
Inputs may be any that keep to these rules, and one draw needn't show every extreme that they name: doc_ids never fall along the sequence; each document has 1 to 2048 tokens, one exactly 2048.
All inputs are finite; a program needn't handle non-finite values.
Results may differ from a plain program's by a relative error of at most 0.019.
Values may be sent and summed in bfloat16 or wider, within the bound.
No kernel may reach another device: no remote copies, remote signals or barrier semaphores. Data moves between devices by JAX's collectives and lax.ppermute only.
A program may use at most 128 MiB of HBM per device.

v0:
```python
import functools
import math

import jax
import jax.numpy as jnp
from jax import lax
from jax.experimental import pallas as pl
from jax.experimental.pallas import tpu as pltpu
from jax.sharding import PartitionSpec as P

HEADS = 64
KVH = 8
HD = 128
GROUP = HEADS // KVH
ROWS = 256
BACK = 8
STEP = 3
STEPS = (BACK + STEP) // STEP
PART = ROWS // 2
QUERY_SCALE = HD ** (-0.5) * math.log2(math.e)
INT_MIN = -(1 << 31)
KEEP_FLIP = 0x1999 + INT_MIN
KEEP_BOUND = (1677722 << 8) + INT_MIN
COLUMNS = 1024
SET_COLUMNS = (((0, 384), (384, 768), (768, 1024)), ((0, 384), (384, 640), (640, 1024)))
LINK_FLIPS = (1, 3, 4)
SET_LINKS = ((0, 1, 2), (1, 2, 0), (2, 0, 1))
MIB = 1 << 20


def xor_shift(value):
    return value ^ lax.shift_right_logical(value, jnp.int32(16))


def mixing(value):
    value = xor_shift(value) * 73244475
    value = xor_shift(value) * 73244475
    return xor_shift(value)


def pack(k, v):
    side = lax.broadcasted_iota(jnp.int32, (2, ROWS, HD), 0)
    return jnp.where(side == 0, k[None], v[None])


def in_hbm(array):
    return pltpu.with_memory_space_constraint(array, pltpu.HBM)


def row_low(starts, row):
    low = jnp.zeros_like(row)
    for v in range(1, 8):
        low = jnp.maximum(low, jnp.where(row >= starts[v], starts[v], 0))
    return low


def slot_flip(slot):
    return (slot & 1) ^ (3 * ((slot >> 1) & 1)) ^ (4 * (slot >> 2))


def prepare_body(seed_ref, docs_hbm, q_hbm, w_hbm, keep, query, weight, starts, docs, q, row_hash, sems):
    ctx = lax.axis_index("ctx")
    tp = lax.axis_index("tp")
    docs_copy = pltpu.make_async_copy(docs_hbm, docs, sems.at[8])
    docs_copy.start()
    q_copy = pltpu.make_async_copy(q_hbm, q, sems.at[9])
    q_copy.start()
    w_copies = []
    for slot in range(8):
        column = pl.multiple_of((tp ^ slot_flip(slot)) * COLUMNS, COLUMNS)
        w_copies.append(
            pltpu.make_async_copy(
                w_hbm.at[:, pl.ds(column, COLUMNS)], weight.at[slot], sems.at[slot]
            )
        )
        w_copies[-1].start()

    row0 = ctx * ROWS
    head0 = tp * GROUP
    seed = seed_ref[0]
    rows = row0 + lax.broadcasted_iota(jnp.int32, (ROWS, 128), 0)
    lanes = lax.broadcasted_iota(jnp.int32, (ROWS, 128), 1)
    for h in range(GROUP):
        head_hash = mixing(jnp.full((8, 128), seed * 7919 + head0 + h, jnp.int32))[:1]
        row_hash[h] = mixing(head_hash ^ (rows * 65537)) + lanes
    docs_copy.wait()
    starts[0] = 0
    for v in range(1, 8):
        starts[v] = jnp.sum((docs[...] < v).astype(jnp.int32))
    n = (row0 - (row_low(starts, row0) & -ROWS)) // ROWS

    def step(t, _):
        for u in range(STEP):
            start = row0 - (STEP * t + u) * ROWS
            used = STEP * t + u <= n

            @pl.when(used)
            def _():
                def head(h, _):
                    for part in range(2):
                        for half in range(2):
                            value = row_hash[h, part * PART : (part + 1) * PART] + (start + half * 128)
                            value = xor_shift(value) * 73244475
                            value = xor_shift(value) * 73244475
                            kept = (value ^ KEEP_FLIP) >= KEEP_BOUND
                            lane = u * ROWS + half * 128
                            keep[t, part, pl.ds(h * PART, PART), lane : lane + 128] = jnp.where(
                                kept, jnp.float32(1), jnp.float32(0)
                            ).astype(jnp.bfloat16)
                    return 0

                lax.fori_loop(0, GROUP, head, 0)

            @pl.when(jnp.logical_not(used))
            def _():
                keep[t, :, :, u * ROWS : (u + 1) * ROWS] = jnp.zeros((2, GROUP * PART, ROWS), jnp.bfloat16)

        return 0

    lax.fori_loop(0, n // STEP + 1, step, 0)
    q_copy.wait()
    for part in range(2):
        for h in range(GROUP):
            scaled = q[part * PART : (part + 1) * PART, h * HD : (h + 1) * HD].astype(jnp.float32)
            scaled = scaled * QUERY_SCALE
            high = scaled.astype(jnp.bfloat16)
            query[part, h * PART : (h + 1) * PART, :HD] = high
            query[part, h * PART : (h + 1) * PART, HD:] = (scaled - high.astype(jnp.float32)).astype(
                jnp.bfloat16
            )
    for copy in w_copies:
        copy.wait()


def prepare(seed, docs, queries, weight):
    vmem = pl.BlockSpec(memory_space=pltpu.VMEM)
    hbm = pl.BlockSpec(memory_space=pltpu.HBM)
    smem = pl.BlockSpec(memory_space=pltpu.SMEM)
    return pl.pallas_call(
        prepare_body,
        out_shape=[
            jax.ShapeDtypeStruct((STEPS, 2, GROUP * PART, STEP * ROWS), jnp.bfloat16),
            jax.ShapeDtypeStruct((2, GROUP * PART, 2 * HD), jnp.bfloat16),
            jax.ShapeDtypeStruct((8, GROUP * HD, COLUMNS), jnp.bfloat16),
            jax.ShapeDtypeStruct((8,), jnp.int32),
        ],
        in_specs=[smem, hbm, hbm, hbm],
        out_specs=[vmem, vmem, vmem, smem],
        scratch_shapes=[
            pltpu.VMEM((32, 128), jnp.int32),
            pltpu.VMEM((ROWS, GROUP * HD), jnp.bfloat16),
            pltpu.VMEM((GROUP, ROWS, 128), jnp.int32),
            pltpu.SemaphoreType.DMA((10,)),
        ],
        compiler_params=pltpu.CompilerParams(vmem_limit_bytes=4 * MIB),
        cost_estimate=pl.CostEstimate(
            flops=400_000_000, bytes_accessed=28 * MIB, transcendentals=0
        ),
        name="prepare",
    )(seed, docs, queries, weight)


def attend_body(part, starts, query, own, other, keep, weight, *refs):
    outs = refs[:6]
    keys, values, score, peak, total, accum, mixed, bias = refs[6:]
    ctx = lax.axis_index("ctx")
    block0 = ctx * ROWS
    row0 = block0 + part * PART
    core = ctx & 1
    n = (block0 - (row_low(starts, block0) & -ROWS)) // ROWS
    last_low = row_low(starts, row0 + PART - 1)

    peak[...] = jnp.full(peak.shape, -3e38, jnp.float32)
    total[...] = jnp.zeros(total.shape, jnp.float32)
    accum[...] = jnp.zeros(accum.shape, jnp.float32)
    for d in range(BACK + 1):
        t, lane = d // STEP, d % STEP * ROWS
        source, at = (other, (d + 1) // 2 - core) if d % 2 else (own, d // 2)
        turned = source[at, 0].T
        keys[t, :HD, lane : lane + ROWS] = turned
        keys[t, HD:, lane : lane + ROWS] = turned
        values[t, lane : lane + ROWS] = source[at, 1]

    def score_step(t, masked):
        value = jnp.dot(query[part], keys[t], preferred_element_type=jnp.float32)
        if masked:
            lane = lax.broadcasted_iota(jnp.int32, (PART, STEP * ROWS), 1)
            key_pos = block0 - STEP * t * ROWS - (lane & -ROWS) + (lane & (ROWS - 1))
            row_pos = row0 + lax.broadcasted_iota(jnp.int32, (PART, 1), 0)
            allowed = (key_pos >= row_low(starts, row_pos)) & (key_pos <= row_pos)
            bias[...] = jnp.where(allowed, jnp.float32(0), jnp.float32(-1e30))
            value = value.reshape(GROUP, PART, STEP * ROWS) + bias[...][None]
            value = value.reshape(GROUP * PART, STEP * ROWS)
        score[t] = value
        top = peak[...]
        for k in range(STEP * ROWS // 128):
            top = jnp.maximum(top, value[:, k * 128 : (k + 1) * 128])
        peak[...] = top

    def score_loop(t, _):
        free = (t > 0) & (block0 - (STEP * t + STEP - 1) * ROWS >= last_low)

        @pl.when(free)
        def _():
            score_step(t, False)

        @pl.when(jnp.logical_not(free))
        def _():
            score_step(t, True)

        return 0

    lax.fori_loop(0, n // STEP + 1, score_loop, 0)
    peak[...] = jnp.broadcast_to(jnp.max(peak[...], axis=1, keepdims=True), peak.shape)

    def value_loop(t, _):
        top = peak[...]
        added = total[...]
        probs = []
        for k in range(STEP * ROWS // 128):
            prob = jnp.exp2(score[t, :, k * 128 : (k + 1) * 128] - top)
            added = added + prob
            probs.append(prob.astype(jnp.bfloat16))
        total[...] = added
        prob = jnp.concatenate(probs, axis=1) * keep[t, part]
        accum[...] = accum[...] + jnp.dot(prob, values[t], preferred_element_type=jnp.float32)
        return 0

    lax.fori_loop(0, n // STEP + 1, value_loop, 0)
    for h in range(GROUP):
        at = slice(h * PART, (h + 1) * PART)
        row_sum = jnp.sum(total[at], axis=1, keepdims=True) * 0.9
        mixed[:, h * HD : (h + 1) * HD] = (accum[at] / row_sum).astype(jnp.bfloat16)

    for slot in range(8):
        product = jnp.dot(mixed[...], weight[slot], preferred_element_type=jnp.float32)
        product = product.astype(jnp.bfloat16)
        bits = [(slot >> k) & 1 for k in range(3)]
        for s, (lo, hi) in enumerate(SET_COLUMNS[part]):
            one, two, three = (bits[k] for k in SET_LINKS[s])
            outs[2 * s + one][2 * two + three] = product[:, lo:hi]


def attend(part, starts, query, own, other, keep, weight):
    vmem = pl.BlockSpec(memory_space=pltpu.VMEM)
    out_shape = []
    for lo, hi in SET_COLUMNS[part]:
        out_shape += [jax.ShapeDtypeStruct((4, PART, hi - lo), jnp.bfloat16)] * 2
    heads_rows = GROUP * PART
    return pl.pallas_call(
        functools.partial(attend_body, part),
        out_shape=out_shape,
        in_specs=[pl.BlockSpec(memory_space=pltpu.SMEM)] + [vmem] * 5,
        out_specs=[vmem] * 6,
        scratch_shapes=[
            pltpu.VMEM((STEPS, 2 * HD, STEP * ROWS), jnp.bfloat16),
            pltpu.VMEM((STEPS, STEP * ROWS, HD), jnp.bfloat16),
            pltpu.VMEM((STEPS, heads_rows, STEP * ROWS), jnp.float32),
            pltpu.VMEM((heads_rows, 128), jnp.float32),
            pltpu.VMEM((heads_rows, 128), jnp.float32),
            pltpu.VMEM((heads_rows, HD), jnp.float32),
            pltpu.VMEM((PART, GROUP * HD), jnp.bfloat16),
            pltpu.VMEM((PART, STEP * ROWS), jnp.float32),
        ],
        compiler_params=pltpu.CompilerParams(vmem_limit_bytes=18 * MIB),
        cost_estimate=pl.CostEstimate(
            flops=3_000_000_000, bytes_accessed=24 * MIB, transcendentals=3_000_000
        ),
        name=f"attend_{part}",
    )(starts, query, own, other, keep, weight)


def swap(array, flip):
    return lax.ppermute(array, "tp", [(i, i ^ flip) for i in range(8)])


def flows(outs):
    return [(outs[2 * s], outs[2 * s + 1]) for s in range(3)]


def exchange(state, step):
    return [swap(state[s][1], LINK_FLIPS[SET_LINKS[s][step]]) for s in range(3)]


def fold(state, got):
    result = []
    for (keep, _), other in zip(state, got):
        held = (keep.astype(jnp.float32) + other.astype(jnp.float32)).astype(jnp.bfloat16)
        half = held.shape[0] // 2
        result.append((held[:half], held[half:]) if half else held[0])
    return result


def after(first, second):
    return lax.optimization_barrier((first, second))


def body(queries, key_proj, value_proj, out_weight, doc_ids, drop_seed):
    own = pack(key_proj, value_proj)
    column = [own]
    for chips in range(1, 5):
        pairs = [(i, (i + 2 * chips) % 16) for i in range(16)]
        column.append(lax.ppermute(own, "ctx", pairs))
    column = jnp.stack(column)
    keep, query, weight, starts = prepare(
        drop_seed, in_hbm(doc_ids.reshape(32, 128)), in_hbm(queries), in_hbm(out_weight)
    )
    column, keep = after(column, keep)
    other = lax.ppermute(column, "ctx", [(i, i ^ 1) for i in range(16)])

    state0 = flows(attend(0, starts, query, column, other, keep, weight))
    got0 = exchange(state0, 0)
    keep, state0 = after(keep, state0)
    state1 = flows(attend(1, starts, query, column, other, keep, weight))
    state1, got0 = after(state1, got0)
    state0 = fold(state0, got0)
    got0 = exchange(state0, 1)
    got1 = exchange(state1, 0)
    state0 = fold(state0, got0)
    state1 = fold(state1, got1)
    state1, state0 = after(state1, state0)
    got0 = exchange(state0, 2)
    got1 = exchange(state1, 1)
    state0 = fold(state0, got0)
    state1 = fold(state1, got1)
    got1 = exchange(state1, 2)
    state1 = fold(state1, got1)
    return jnp.concatenate(
        [jnp.concatenate(state0, axis=1), jnp.concatenate(state1, axis=1)], axis=0
    )


def solution(mesh):
    in_specs = (P("ctx", "tp"), P("ctx", "tp"), P("ctx", "tp"), P("tp", None), P(), P())
    return jax.shard_map(
        body, mesh=mesh, in_specs=in_specs, out_specs=P("ctx", "tp"), check_vma=False
    )
```

profile of v0, /device:TPU:18, one launch (start us, length us, event | category | flops | bytes accessed | tf_op | source)
XLA Modules:
  0.0 78.7 jit_solution(754969060760951903)
XLA Ops:
  0.0 1.0 %broadcast_select_fusion = bf16[2,256,128]{2,1,0:T(8,128)(2,1)S(1)} fusion(pred[2]{0:T(512)(128)(4,1)S(1)} %iota_compare_fusion, bf16[256,128]{1,0:T(8,128)(2,1)} %param.8, bf16[256,128]{1,0:T(8,128)(2,1)} %param.7), kind=kLoop, calls=%fused_computation.24 | loop fusion | flops 65536 | bytes 262146 | tf_op jit(solution)/shard_map/jit(_where)/select_n | solution.py:43
  1.0 2.2 %collective-permute-start.3 = (bf16[2,256,128]{2,1,0:T(8,128)(2,1)S(1)}, bf16[2,256,128]{2,1,0:T(8,128)(2,1)S(1)}, u32[]{:S(2)}, u32[]{:S(2)}) collective-permute-start(bf16[2,256,128]{2,1,0:T(8,128)(2,1)S(1)} %broadcast_select_fusion), channel_id=1, source_target_pairs={{0,64},{8,72},{16,80},{24,88},{32,96},{40,104},{48,112},{56,120},{... | collective-permute-start | bytes 393224 | tf_op jit(solution)/shard_map/ppermute | solution.py:303
  3.2 1.2 %collective-permute-start.2 = (bf16[2,256,128]{2,1,0:T(8,128)(2,1)S(1)}, bf16[2,256,128]{2,1,0:T(8,128)(2,1)S(1)}, u32[]{:S(2)}, u32[]{:S(2)}) collective-permute-start(bf16[2,256,128]{2,1,0:T(8,128)(2,1)S(1)} %broadcast_select_fusion), channel_id=1, source_target_pairs={{0,48},{8,56},{16,64},{24,72},{32,80},{40,88},{48,96},{56,104},{64... | collective-permute-start | bytes 393224 | tf_op jit(solution)/shard_map/ppermute | solution.py:303
  4.3 1.5 %collective-permute-start.1 = (bf16[2,256,128]{2,1,0:T(8,128)(2,1)S(1)}, bf16[2,256,128]{2,1,0:T(8,128)(2,1)S(1)}, u32[]{:S(2)}, u32[]{:S(2)}) collective-permute-start(bf16[2,256,128]{2,1,0:T(8,128)(2,1)S(1)} %broadcast_select_fusion), channel_id=1, source_target_pairs={{0,32},{8,40},{16,48},{24,56},{32,64},{40,72},{48,80},{56,88},{64,... | collective-permute-start | bytes 393224 | tf_op jit(solution)/shard_map/ppermute | solution.py:303
  5.8 3.8 %collective-permute-start = (bf16[2,256,128]{2,1,0:T(8,128)(2,1)S(1)}, bf16[2,256,128]{2,1,0:T(8,128)(2,1)S(1)}, u32[]{:S(2)}, u32[]{:S(2)}) collective-permute-start(bf16[2,256,128]{2,1,0:T(8,128)(2,1)S(1)} %broadcast_select_fusion), channel_id=1, source_target_pairs={{0,16},{8,24},{16,32},{24,40},{32,48},{40,56},{48,64},{56,72},{64,... | collective-permute-start | bytes 393224 | tf_op jit(solution)/shard_map/ppermute | solution.py:303
  9.6 1.0 %select_dynamic-update-slice_fusion = bf16[5,2,256,128]{3,2,1,0:T(8,128)(2,1)S(1)} fusion(pred[2]{0:T(512)(128)(4,1)S(1)} %iota_compare_fusion, bf16[256,128]{1,0:T(8,128)(2,1)} %param.8, bf16[256,128]{1,0:T(8,128)(2,1)} %param.7), kind=kLoop, calls=%fused_computation.23 | loop fusion | flops 65535 | bytes 262146
  11.3 6.8 %prepare.1 = (bf16[3,2,1024,768]{3,2,1,0:T(8,128)(2,1)S(1)}, bf16[2,1024,256]{2,1,0:T(8,128)(2,1)S(1)}, bf16[8,1024,1024]{2,1,0:T(8,128)(2,1)S(1)}, s32[8]{0:T(128)S(1)}) custom-call(s32[1]{0:T(128)S(6)} %copy.11.seed_ref, s32[32,128]{1,0:T(8,128)} %bitcast.21, bf16[256,1024]{1,0:T(8,128)(2,1)} %q_hbm.1, bf16[1024,8192]{1,0:T(8,128)(2,1)} %w_hbm.1), custom_call_target="tpu_custom_call" | custom-call | flops 400000000 | bytes 29360128 | tf_op jit(solution)/shard_map/prepare/pallas_call | solution.py:139
  18.3 2.1 %collective-permute-done.4.other = bf16[5,2,256,128]{3,2,1,0:T(8,128)(2,1)S(1)} collective-permute-done((bf16[5,2,256,128]{3,2,1,0:T(8,128)(2,1)S(1)}, bf16[5,2,256,128]{3,2,1,0:T(8,128)(2,1)S(1)}, u32[]{:S(2)}, u32[]{:S(2)}) %collective-permute-start.4) | collective-permute-done | bytes 655392 | tf_op jit(solution)/shard_map/ppermute | solution.py:309
  20.4 6.3 %attend_0.1 = (bf16[4,128,384]{2,1,0:T(8,128)(2,1)S(1)}, bf16[4,128,384]{2,1,0:T(8,128)(2,1)S(1)}, bf16[4,128,384]{2,1,0:T(8,128)(2,1)S(1)}, bf16[4,128,384]{2,1...) custom-call(s32[8]{0:T(128)S(1)} %get-tuple-element.48.starts, ...), custom_call_target="tpu_custom_call" | custom-call | flops 3000000000 | bytes 25165824 | tf_op jit(solution)/shard_map/attend_0/pallas_call | solution.py:250
  26.7 2.0 %collective-permute-start.5 = (bf16[4,128,384]{2,1,0:T(8,128)(2,1)S(1)}, bf16[4,128,384]{2,1,0:T(8,128)(2,1)S(1)}, u32[]{:S(2)}, u32[]{:S(2)}) collective-permute-start(bf16[4,128,384]{2,1,0:T(8,128)(2,1)S(1)} %get-tuple-element.55), channel_id=1, source_target_pairs={{0,1},{1,0},{2,3},{3,2},{4,5},{5,4},{6,7},{7,6},{8,9},{9,8},{10,11... | collective-permute-start | bytes 1179656 | tf_op jit(solution)/shard_map/ppermute | solution.py:274
  28.7 2.5 %collective-permute-start.6 = (bf16[4,128,384]{2,1,0:T(8,128)(2,1)S(1)}, bf16[4,128,384]{2,1,0:T(8,128)(2,1)S(1)}, u32[]{:S(2)}, u32[]{:S(2)}) collective-permute-start(bf16[4,128,384]{2,1,0:T(8,128)(2,1)S(1)} %get-tuple-element.57), channel_id=1, source_target_pairs={{0,3},{1,2},{2,1},{3,0},{4,7},{5,6},{6,5},{7,4},{8,11},{9,10},{10,... | collective-permute-start | bytes 1179656 | tf_op jit(solution)/shard_map/ppermute | solution.py:274
  31.2 1.3 %collective-permute-start.7 = (bf16[4,128,256]{2,1,0:T(8,128)(2,1)S(1)}, bf16[4,128,256]{2,1,0:T(8,128)(2,1)S(1)}, u32[]{:S(2)}, u32[]{:S(2)}) collective-permute-start(bf16[4,128,256]{2,1,0:T(8,128)(2,1)S(1)} %get-tuple-element.59), channel_id=1, source_target_pairs={{0,4},{1,5},{2,6},{3,7},{4,0},{5,1},{6,2},{7,3},{8,12},{9,13},{10,... | collective-permute-start | bytes 786440 | tf_op jit(solution)/shard_map/ppermute | solution.py:274
  32.5 6.5 %attend_1.1 = (bf16[4,128,384]{2,1,0:T(8,128)(2,1)S(1)}, bf16[4,128,384]{2,1,0:T(8,128)(2,1)S(1)}, bf16[4,128,256]{2,1,0:T(8,128)(2,1)S(1)}, bf16[4,128,256]{2,1...) custom-call(s32[8]{0:T(128)S(1)} %get-tuple-element.48.starts, ...), custom_call_target="tpu_custom_call" | custom-call | flops 3000000000 | bytes 25165824 | tf_op jit(solution)/shard_map/attend_1/pallas_call | solution.py:250
  39.0 1.3 %collective-permute-done.7 = bf16[4,128,256]{2,1,0:T(8,128)(2,1)S(1)} collective-permute-done((bf16[4,128,256]{2,1,0:T(8,128)(2,1)S(1)}, bf16[4,128,256]{2,1,0:T(8,128)(2,1)S(1)}, u32[]{:S(2)}, u32[]{:S(2)}) %collective-permute-start.7) | collective-permute-done | bytes 262176 | tf_op jit(solution)/shard_map/ppermute | solution.py:274
  40.3 1.4 %collective-permute-done.6 = bf16[4,128,384]{2,1,0:T(8,128)(2,1)S(1)} collective-permute-done((bf16[4,128,384]{2,1,0:T(8,128)(2,1)S(1)}, bf16[4,128,384]{2,1,0:T(8,128)(2,1)S(1)}, u32[]{:S(2)}, u32[]{:S(2)}) %collective-permute-start.6) | collective-permute-done | bytes 393248 | tf_op jit(solution)/shard_map/ppermute | solution.py:274
  42.2 1.4 %collective-permute-start.12 = (bf16[2,128,384]{2,1,0:T(8,128)(2,1)S(1)}, bf16[2,128,384]{2,1,0:T(8,128)(2,1)S(1)}, u32[]{:S(2)}, u32[]{:S(2)}) collective-permute-start(bf16[2,128,384]{2,1,0:T(8,128)(2,1)S(1)} %slice.107), channel_id=1, source_target_pairs={{0,4},{1,5},{2,6},{3,7},{4,0},{5,1},{6,2},{7,3},{8,12},{9,13},{10,... | collective-permute-start | bytes 589832 | tf_op jit(solution)/shard_map/ppermute | solution.py:274
  43.6 2.8 %collective-permute-start.11 = (bf16[2,128,384]{2,1,0:T(8,128)(2,1)S(1)}, bf16[2,128,384]{2,1,0:T(8,128)(2,1)S(1)}, u32[]{:S(2)}, u32[]{:S(2)}) collective-permute-start(bf16[2,128,384]{2,1,0:T(8,128)(2,1)S(1)} %slice.103), channel_id=1, source_target_pairs={{0,3},{1,2},{2,1},{3,0},{4,7},{5,6},{6,5},{7,4},{8,11},{9,10},{10,... | collective-permute-start | bytes 589832 | tf_op jit(solution)/shard_map/ppermute | solution.py:274
  47.6 1.1 %collective-permute-start.10 = (bf16[4,128,384]{2,1,0:T(8,128)(2,1)S(1)}, bf16[4,128,384]{2,1,0:T(8,128)(2,1)S(1)}, u32[]{:S(2)}, u32[]{:S(2)}) collective-permute-start(bf16[4,128,384]{2,1,0:T(8,128)(2,1)S(1)} %get-tuple-element.72), channel_id=1, source_target_pairs={{0,4},{1,5},{2,6},{3,7},{4,0},{5,1},{6,2},{7,3},{8,12},{9,13},{10,... | collective-permute-start | bytes 1179656 | tf_op jit(solution)/shard_map/ppermute | solution.py:274
  49.2 3.4 %collective-permute-done.11 = bf16[2,128,384]{2,1,0:T(8,128)(2,1)S(1)} collective-permute-done((bf16[2,128,384]{2,1,0:T(8,128)(2,1)S(1)}, bf16[2,128,384]{2,1,0:T(8,128)(2,1)S(1)}, u32[]{:S(2)}, u32[]{:S(2)}) %collective-permute-start.11) | collective-permute-done | bytes 196640 | tf_op jit(solution)/shard_map/ppermute | solution.py:274
  52.7 4.3 %collective-permute-done.9 = bf16[4,128,256]{2,1,0:T(8,128)(2,1)S(1)} collective-permute-done((bf16[4,128,256]{2,1,0:T(8,128)(2,1)S(1)}, bf16[4,128,256]{2,1,0:T(8,128)(2,1)S(1)}, u32[]{:S(2)}, u32[]{:S(2)}) %collective-permute-start.9) | collective-permute-done | bytes 262176 | tf_op jit(solution)/shard_map/ppermute | solution.py:274
  57.8 2.6 %collective-permute-start.16 = (bf16[1,128,256]{2,1,0:T(8,128)(2,1)S(1)}, bf16[1,128,256]{2,1,0:T(8,128)(2,1)S(1)}, u32[]{:S(2)}, u32[]{:S(2)}) collective-permute-start(bf16[1,128,256]{2,1,0:T(8,128)(2,1)S(1)} %get-tuple-element.84), channel_id=1, source_target_pairs={{0,3},{1,2},{2,1},{3,0},{4,7},{5,6},{6,5},{7,4},{8,11},{9,10},{10,... | collective-permute-start | bytes 196616 | tf_op jit(solution)/shard_map/ppermute | solution.py:274
  60.4 1.3 %collective-permute-start.14 = (bf16[1,128,384]{2,1,0:T(8,128)(2,1)S(1)}, bf16[1,128,384]{2,1,0:T(8,128)(2,1)S(1)}, u32[]{:S(2)}, u32[]{:S(2)}) collective-permute-start(bf16[1,128,384]{2,1,0:T(8,128)(2,1)S(1)} %get-tuple-element.80), channel_id=1, source_target_pairs={{0,4},{1,5},{2,6},{3,7},{4,0},{5,1},{6,2},{7,3},{8,12},{9,13},{10,... | collective-permute-start | bytes 294920 | tf_op jit(solution)/shard_map/ppermute | solution.py:274
  61.7 1.0 %collective-permute-start.15 = (bf16[1,128,384]{2,1,0:T(8,128)(2,1)S(1)}, bf16[1,128,384]{2,1,0:T(8,128)(2,1)S(1)}, u32[]{:S(2)}, u32[]{:S(2)}) collective-permute-start(bf16[1,128,384]{2,1,0:T(8,128)(2,1)S(1)} %get-tuple-element.82), channel_id=1, source_target_pairs={{0,1},{1,0},{2,3},{3,2},{4,5},{5,4},{6,7},{7,6},{8,9},{9,8},{10,11... | collective-permute-start | bytes 294920 | tf_op jit(solution)/shard_map/ppermute | solution.py:274
  64.6 1.1 %collective-permute-done.14 = bf16[1,128,384]{2,1,0:T(8,128)(2,1)S(1)} collective-permute-done((bf16[1,128,384]{2,1,0:T(8,128)(2,1)S(1)}, bf16[1,128,384]{2,1,0:T(8,128)(2,1)S(1)}, u32[]{:S(2)}, u32[]{:S(2)}) %collective-permute-start.14) | collective-permute-done | bytes 98336 | tf_op jit(solution)/shard_map/ppermute | solution.py:274
  65.7 1.5 %collective-permute-done.15 = bf16[1,128,384]{2,1,0:T(8,128)(2,1)S(1)} collective-permute-done((bf16[1,128,384]{2,1,0:T(8,128)(2,1)S(1)}, bf16[1,128,384]{2,1,0:T(8,128)(2,1)S(1)}, u32[]{:S(2)}, u32[]{:S(2)}) %collective-permute-start.15) | collective-permute-done | bytes 98336 | tf_op jit(solution)/shard_map/ppermute | solution.py:274
  67.8 1.1 %collective-permute-start.20 = (bf16[1,128,256]{2,1,0:T(8,128)(2,1)S(1)}, bf16[1,128,256]{2,1,0:T(8,128)(2,1)S(1)}, u32[]{:S(2)}, u32[]{:S(2)}) collective-permute-start(bf16[1,128,256]{2,1,0:T(8,128)(2,1)S(1)} %slice.117), channel_id=1, source_target_pairs={{0,1},{1,0},{2,3},{3,2},{4,5},{5,4},{6,7},{7,6},{8,9},{9,8},{10,11... | collective-permute-start | bytes 196616 | tf_op jit(solution)/shard_map/ppermute | solution.py:274
  68.9 1.5 %collective-permute-done.17 = bf16[2,128,384]{2,1,0:T(8,128)(2,1)S(1)} collective-permute-done((bf16[2,128,384]{2,1,0:T(8,128)(2,1)S(1)}, bf16[2,128,384]{2,1,0:T(8,128)(2,1)S(1)}, u32[]{:S(2)}, u32[]{:S(2)}) %collective-permute-start.17) | collective-permute-done | bytes 196640 | tf_op jit(solution)/shard_map/ppermute | solution.py:274
  70.4 1.4 %collective-permute-start.18 = (bf16[1,128,384]{2,1,0:T(8,128)(2,1)S(1)}, bf16[1,128,384]{2,1,0:T(8,128)(2,1)S(1)}, u32[]{:S(2)}, u32[]{:S(2)}) collective-permute-start(bf16[1,128,384]{2,1,0:T(8,128)(2,1)S(1)} %slice.115), channel_id=1, source_target_pairs={{0,4},{1,5},{2,6},{3,7},{4,0},{5,1},{6,2},{7,3},{8,12},{9,13},{10,... | collective-permute-start | bytes 294920 | tf_op jit(solution)/shard_map/ppermute | solution.py:274
  71.9 0.8 collective-permute-start.22
  72.7 2.4 %collective-permute-done.18 = bf16[1,128,384]{2,1,0:T(8,128)(2,1)S(1)} collective-permute-done((bf16[1,128,384]{2,1,0:T(8,128)(2,1)S(1)}, bf16[1,128,384]{2,1,0:T(8,128)(2,1)S(1)}, u32[]{:S(2)}, u32[]{:S(2)}) %collective-permute-start.18) | collective-permute-done | bytes 98336 | tf_op jit(solution)/shard_map/ppermute | solution.py:274
  75.2 2.6 %collective-permute-done.22 = bf16[1,128,384]{2,1,0:T(8,128)(2,1)S(1)} collective-permute-done((bf16[1,128,384]{2,1,0:T(8,128)(2,1)S(1)}, bf16[1,128,384]{2,1,0:T(8,128)(2,1)S(1)}, u32[]{:S(2)}, u32[]{:S(2)}) %collective-permute-start.22) | collective-permute-done | bytes 98336 | tf_op jit(solution)/shard_map/ppermute | solution.py:274
  77.8 0.9 %maximum_maximum_fusion = bf16[256,1024]{1,0:T(8,128)(2,1)} fusion(bf16[128,384]{1,0:T(8,128)(2,1)S(1)} %fusion.3, bf16[128,256]{1,0:T(8,128)(2,1)S(1)} %fusion.5, bf16[128,384]{1,0:T(8,128)(2,1)S(1)} %fusion.2, bf16[128,256]{1,0:T(8,128)(2,1)S(1)} %fusion.4, bf16[128,384]{1,0:T(8,128)(2,1)S(1)} %fusion.1, bf16[128,384]{1,0:T(8,128)(2,1)S(1)} %fusion), kind=kLoop, calls=%fused_computation.4 | loop fusion | flops 3145728 | bytes 1048576 | tf_op jit(solution)/shard_map/concatenate | solution.py:328
  (55 shorter events, 5.9 us)
Async XLA Ops:
  1.0 17.2 %collective-permute-start.3 = (bf16[2,256,128]{2,1,0:T(8,128)(2,1)S(1)}, bf16[2,256,128]{2,1,0:T(8,128)(2,1)S(1)}, u32[]{:S(2)}, u32[]{:S(2)}) collective-permute-start(bf16[2,256,128]{2,1,0:T(8,128)(2,1)S(1)} %broadcast_select_fusion), channel_id=1, source_target_pairs={{0,64},{8,72},{16,80},{24,88},{32,96},{40,104},{48,112},{56,120},{... | collective-permute-start | bytes 393224 | tf_op jit(solution)/shard_map/ppermute | solution.py:303
  3.2 15.0 %collective-permute-start.2 = (bf16[2,256,128]{2,1,0:T(8,128)(2,1)S(1)}, bf16[2,256,128]{2,1,0:T(8,128)(2,1)S(1)}, u32[]{:S(2)}, u32[]{:S(2)}) collective-permute-start(bf16[2,256,128]{2,1,0:T(8,128)(2,1)S(1)} %broadcast_select_fusion), channel_id=1, source_target_pairs={{0,48},{8,56},{16,64},{24,72},{32,80},{40,88},{48,96},{56,104},{64... | collective-permute-start | bytes 393224 | tf_op jit(solution)/shard_map/ppermute | solution.py:303
  4.3 13.7 %collective-permute-start.1 = (bf16[2,256,128]{2,1,0:T(8,128)(2,1)S(1)}, bf16[2,256,128]{2,1,0:T(8,128)(2,1)S(1)}, u32[]{:S(2)}, u32[]{:S(2)}) collective-permute-start(bf16[2,256,128]{2,1,0:T(8,128)(2,1)S(1)} %broadcast_select_fusion), channel_id=1, source_target_pairs={{0,32},{8,40},{16,48},{24,56},{32,64},{40,72},{48,80},{56,88},{64,... | collective-permute-start | bytes 393224 | tf_op jit(solution)/shard_map/ppermute | solution.py:303
  5.8 12.2 %collective-permute-start = (bf16[2,256,128]{2,1,0:T(8,128)(2,1)S(1)}, bf16[2,256,128]{2,1,0:T(8,128)(2,1)S(1)}, u32[]{:S(2)}, u32[]{:S(2)}) collective-permute-start(bf16[2,256,128]{2,1,0:T(8,128)(2,1)S(1)} %broadcast_select_fusion), channel_id=1, source_target_pairs={{0,16},{8,24},{16,32},{24,40},{32,48},{40,56},{48,64},{56,72},{64,... | collective-permute-start | bytes 393224 | tf_op jit(solution)/shard_map/ppermute | solution.py:303
  18.2 2.2 %collective-permute-start.4 = (bf16[5,2,256,128]{3,2,1,0:T(8,128)(2,1)S(1)}, bf16[5,2,256,128]{3,2,1,0:T(8,128)(2,1)S(1)}, u32[]{:S(2)}, u32[]{:S(2)}) collective-permute-start(bf16[5,2,256,128]{3,2,1,0:T(8,128)(2,1)S(1)} %bitcast_dynamic-update-slice_fusion.own), channel_id=1, source_target_pairs={{0,8},{8,0},{16,24},{24,16},{32,40},{40,32},{48,56},{56,48},{64,72... | collective-permute-start | bytes 1966088 | tf_op jit(solution)/shard_map/ppermute | solution.py:309
  26.7 13.6 %collective-permute-start.5 = (bf16[4,128,384]{2,1,0:T(8,128)(2,1)S(1)}, bf16[4,128,384]{2,1,0:T(8,128)(2,1)S(1)}, u32[]{:S(2)}, u32[]{:S(2)}) collective-permute-start(bf16[4,128,384]{2,1,0:T(8,128)(2,1)S(1)} %get-tuple-element.55), channel_id=1, source_target_pairs={{0,1},{1,0},{2,3},{3,2},{4,5},{5,4},{6,7},{7,6},{8,9},{9,8},{10,11... | collective-permute-start | bytes 1179656 | tf_op jit(solution)/shard_map/ppermute | solution.py:274
  28.7 13.0 %collective-permute-start.6 = (bf16[4,128,384]{2,1,0:T(8,128)(2,1)S(1)}, bf16[4,128,384]{2,1,0:T(8,128)(2,1)S(1)}, u32[]{:S(2)}, u32[]{:S(2)}) collective-permute-start(bf16[4,128,384]{2,1,0:T(8,128)(2,1)S(1)} %get-tuple-element.57), channel_id=1, source_target_pairs={{0,3},{1,2},{2,1},{3,0},{4,7},{5,6},{6,5},{7,4},{8,11},{9,10},{10,... | collective-permute-start | bytes 1179656 | tf_op jit(solution)/shard_map/ppermute | solution.py:274
  31.2 9.1 %collective-permute-start.7 = (bf16[4,128,256]{2,1,0:T(8,128)(2,1)S(1)}, bf16[4,128,256]{2,1,0:T(8,128)(2,1)S(1)}, u32[]{:S(2)}, u32[]{:S(2)}) collective-permute-start(bf16[4,128,256]{2,1,0:T(8,128)(2,1)S(1)} %get-tuple-element.59), channel_id=1, source_target_pairs={{0,4},{1,5},{2,6},{3,7},{4,0},{5,1},{6,2},{7,3},{8,12},{9,13},{10,... | collective-permute-start | bytes 786440 | tf_op jit(solution)/shard_map/ppermute | solution.py:274
  41.8 5.8 %collective-permute-start.13 = (bf16[2,128,256]{2,1,0:T(8,128)(2,1)S(1)}, bf16[2,128,256]{2,1,0:T(8,128)(2,1)S(1)}, u32[]{:S(2)}, u32[]{:S(2)}) collective-permute-start(bf16[2,128,256]{2,1,0:T(8,128)(2,1)S(1)} %slice.111), channel_id=1, source_target_pairs={{0,1},{1,0},{2,3},{3,2},{4,5},{5,4},{6,7},{7,6},{8,9},{9,8},{10,11... | collective-permute-start | bytes 393224 | tf_op jit(solution)/shard_map/ppermute | solution.py:274
  42.2 6.9 %collective-permute-start.12 = (bf16[2,128,384]{2,1,0:T(8,128)(2,1)S(1)}, bf16[2,128,384]{2,1,0:T(8,128)(2,1)S(1)}, u32[]{:S(2)}, u32[]{:S(2)}) collective-permute-start(bf16[2,128,384]{2,1,0:T(8,128)(2,1)S(1)} %slice.107), channel_id=1, source_target_pairs={{0,4},{1,5},{2,6},{3,7},{4,0},{5,1},{6,2},{7,3},{8,12},{9,13},{10,... | collective-permute-start | bytes 589832 | tf_op jit(solution)/shard_map/ppermute | solution.py:274
  43.6 9.0 %collective-permute-start.11 = (bf16[2,128,384]{2,1,0:T(8,128)(2,1)S(1)}, bf16[2,128,384]{2,1,0:T(8,128)(2,1)S(1)}, u32[]{:S(2)}, u32[]{:S(2)}) collective-permute-start(bf16[2,128,384]{2,1,0:T(8,128)(2,1)S(1)} %slice.103), channel_id=1, source_target_pairs={{0,3},{1,2},{2,1},{3,0},{4,7},{5,6},{6,5},{7,4},{8,11},{9,10},{10,... | collective-permute-start | bytes 589832 | tf_op jit(solution)/shard_map/ppermute | solution.py:274
  46.4 10.6 %collective-permute-start.9 = (bf16[4,128,256]{2,1,0:T(8,128)(2,1)S(1)}, bf16[4,128,256]{2,1,0:T(8,128)(2,1)S(1)}, u32[]{:S(2)}, u32[]{:S(2)}) collective-permute-start(bf16[4,128,256]{2,1,0:T(8,128)(2,1)S(1)} %get-tuple-element.70), channel_id=1, source_target_pairs={{0,3},{1,2},{2,1},{3,0},{4,7},{5,6},{6,5},{7,4},{8,11},{9,10},{10,... | collective-permute-start | bytes 786440 | tf_op jit(solution)/shard_map/ppermute | solution.py:274
  46.8 10.3 %collective-permute-start.8 = (bf16[4,128,384]{2,1,0:T(8,128)(2,1)S(1)}, bf16[4,128,384]{2,1,0:T(8,128)(2,1)S(1)}, u32[]{:S(2)}, u32[]{:S(2)}) collective-permute-start(bf16[4,128,384]{2,1,0:T(8,128)(2,1)S(1)} %get-tuple-element.68), channel_id=1, source_target_pairs={{0,1},{1,0},{2,3},{3,2},{4,5},{5,4},{6,7},{7,6},{8,9},{9,8},{10,11... | collective-permute-start | bytes 1179656 | tf_op jit(solution)/shard_map/ppermute | solution.py:274
  47.6 10.1 %collective-permute-start.10 = (bf16[4,128,384]{2,1,0:T(8,128)(2,1)S(1)}, bf16[4,128,384]{2,1,0:T(8,128)(2,1)S(1)}, u32[]{:S(2)}, u32[]{:S(2)}) collective-permute-start(bf16[4,128,384]{2,1,0:T(8,128)(2,1)S(1)} %get-tuple-element.72), channel_id=1, source_target_pairs={{0,4},{1,5},{2,6},{3,7},{4,0},{5,1},{6,2},{7,3},{8,12},{9,13},{10,... | collective-permute-start | bytes 1179656 | tf_op jit(solution)/shard_map/ppermute | solution.py:274
  57.8 6.4 %collective-permute-start.16 = (bf16[1,128,256]{2,1,0:T(8,128)(2,1)S(1)}, bf16[1,128,256]{2,1,0:T(8,128)(2,1)S(1)}, u32[]{:S(2)}, u32[]{:S(2)}) collective-permute-start(bf16[1,128,256]{2,1,0:T(8,128)(2,1)S(1)} %get-tuple-element.84), channel_id=1, source_target_pairs={{0,3},{1,2},{2,1},{3,0},{4,7},{5,6},{6,5},{7,4},{8,11},{9,10},{10,... | collective-permute-start | bytes 196616 | tf_op jit(solution)/shard_map/ppermute | solution.py:274
  60.4 5.3 %collective-permute-start.14 = (bf16[1,128,384]{2,1,0:T(8,128)(2,1)S(1)}, bf16[1,128,384]{2,1,0:T(8,128)(2,1)S(1)}, u32[]{:S(2)}, u32[]{:S(2)}) collective-permute-start(bf16[1,128,384]{2,1,0:T(8,128)(2,1)S(1)} %get-tuple-element.80), channel_id=1, source_target_pairs={{0,4},{1,5},{2,6},{3,7},{4,0},{5,1},{6,2},{7,3},{8,12},{9,13},{10,... | collective-permute-start | bytes 294920 | tf_op jit(solution)/shard_map/ppermute | solution.py:274
  61.7 5.5 %collective-permute-start.15 = (bf16[1,128,384]{2,1,0:T(8,128)(2,1)S(1)}, bf16[1,128,384]{2,1,0:T(8,128)(2,1)S(1)}, u32[]{:S(2)}, u32[]{:S(2)}) collective-permute-start(bf16[1,128,384]{2,1,0:T(8,128)(2,1)S(1)} %get-tuple-element.82), channel_id=1, source_target_pairs={{0,1},{1,0},{2,3},{3,2},{4,5},{5,4},{6,7},{7,6},{8,9},{9,8},{10,11... | collective-permute-start | bytes 294920 | tf_op jit(solution)/shard_map/ppermute | solution.py:274
  62.8 5.0 %collective-permute-start.19 = (bf16[2,128,256]{2,1,0:T(8,128)(2,1)S(1)}, bf16[2,128,256]{2,1,0:T(8,128)(2,1)S(1)}, u32[]{:S(2)}, u32[]{:S(2)}) collective-permute-start(bf16[2,128,256]{2,1,0:T(8,128)(2,1)S(1)} %get-tuple-element.88), channel_id=1, source_target_pairs={{0,4},{1,5},{2,6},{3,7},{4,0},{5,1},{6,2},{7,3},{8,12},{9,13},{10,... | collective-permute-start | bytes 393224 | tf_op jit(solution)/shard_map/ppermute | solution.py:274
  63.5 6.9 %collective-permute-start.17 = (bf16[2,128,384]{2,1,0:T(8,128)(2,1)S(1)}, bf16[2,128,384]{2,1,0:T(8,128)(2,1)S(1)}, u32[]{:S(2)}, u32[]{:S(2)}) collective-permute-start(bf16[2,128,384]{2,1,0:T(8,128)(2,1)S(1)} %get-tuple-element.86), channel_id=1, source_target_pairs={{0,3},{1,2},{2,1},{3,0},{4,7},{5,6},{6,5},{7,4},{8,11},{9,10},{10,... | collective-permute-start | bytes 589832 | tf_op jit(solution)/shard_map/ppermute | solution.py:274
  64.2 7.6 %collective-permute-start.21 = (bf16[2,128,384]{2,1,0:T(8,128)(2,1)S(1)}, bf16[2,128,384]{2,1,0:T(8,128)(2,1)S(1)}, u32[]{:S(2)}, u32[]{:S(2)}) collective-permute-start(bf16[2,128,384]{2,1,0:T(8,128)(2,1)S(1)} %get-tuple-element.90), channel_id=1, source_target_pairs={{0,1},{1,0},{2,3},{3,2},{4,5},{5,4},{6,7},{7,6},{8,9},{9,8},{10,11... | collective-permute-start | bytes 589832 | tf_op jit(solution)/shard_map/ppermute | solution.py:274
  67.8 4.9 %collective-permute-start.20 = (bf16[1,128,256]{2,1,0:T(8,128)(2,1)S(1)}, bf16[1,128,256]{2,1,0:T(8,128)(2,1)S(1)}, u32[]{:S(2)}, u32[]{:S(2)}) collective-permute-start(bf16[1,128,256]{2,1,0:T(8,128)(2,1)S(1)} %slice.117), channel_id=1, source_target_pairs={{0,1},{1,0},{2,3},{3,2},{4,5},{5,4},{6,7},{7,6},{8,9},{9,8},{10,11... | collective-permute-start | bytes 196616 | tf_op jit(solution)/shard_map/ppermute | solution.py:274
  70.4 4.7 %collective-permute-start.18 = (bf16[1,128,384]{2,1,0:T(8,128)(2,1)S(1)}, bf16[1,128,384]{2,1,0:T(8,128)(2,1)S(1)}, u32[]{:S(2)}, u32[]{:S(2)}) collective-permute-start(bf16[1,128,384]{2,1,0:T(8,128)(2,1)S(1)} %slice.115), channel_id=1, source_target_pairs={{0,4},{1,5},{2,6},{3,7},{4,0},{5,1},{6,2},{7,3},{8,12},{9,13},{10,... | collective-permute-start | bytes 294920 | tf_op jit(solution)/shard_map/ppermute | solution.py:274
  71.9 5.9 %collective-permute-start.22 = (bf16[1,128,384]{2,1,0:T(8,128)(2,1)S(1)}, bf16[1,128,384]{2,1,0:T(8,128)(2,1)S(1)}, u32[]{:S(2)}, u32[]{:S(2)}) collective-permute-start(bf16[1,128,384]{2,1,0:T(8,128)(2,1)S(1)} %slice.119), channel_id=1, source_target_pairs={{0,3},{1,2},{2,1},{3,0},{4,7},{5,6},{6,5},{7,4},{8,11},{9,10},{10,... | collective-permute-start | bytes 294920 | tf_op jit(solution)/shard_map/ppermute | solution.py:274
where the time goes:
time: 78.7 us
  starting transfers between devices  31.1 us (40%)
  waiting for transfers between devices  23 us (29%)
  Pallas kernels  19.5 us (25%)
  other arithmetic  3.75 us (5%)
  between operations  0.94 us (1%)
    ppermute x18, starting transfers between devices, swap(): return lax.ppermute(array, 'tp', [(i, i ^ flip) for i in range(8)])  22.4 us
    ppermute x18, waiting for transfers between devices, swap(): return lax.ppermute(array, 'tp', [(i, i ^ flip) for i in range(8)])  20.9 us
    pallas_call x2, Pallas kernels, attend(): pl.pallas_call(functools.partial(attend_body, part), out_shape=out_shape,...  12.8 us
    ppermute x4, starting transfers between devices, body(): column.append(lax.ppermute(own, 'ctx', pairs))  8.67 us
    pallas_call x1, Pallas kernels, prepare(): pl.pallas_call(prepare_body, out_shape=[jax.ShapeDtypeStruct((STEPS, 2, G...  6.78 us
    ppermute x1, waiting for transfers between devices, body(): other = lax.ppermute(column, 'ctx', [(i, i ^ 1) for i in range(16)])  2.08 us
  transfers between devices with their start and end apart: 23, of which 13 were waited for; matrix products, arithmetic and copies ran while one was open for 3% of the time, Pallas kernels for 17%

commit v1 on v0

v1 whole, which is shorter than its diff:
```python
import functools
import math

import jax
import jax.numpy as jnp
from jax import lax
from jax.experimental import pallas as pl
from jax.experimental.pallas import tpu as pltpu
from jax.sharding import PartitionSpec as P

HEADS = 64
KVH = 8
HD = 128
GROUP = HEADS // KVH
ROWS = 256
BACK = 8
STEP = 3
STEPS = (BACK + STEP) // STEP
QUERY_SCALE = HD ** (-0.5) * math.log2(math.e)
INT_MIN = -(1 << 31)
KEEP_FLIP = 0x1999 + INT_MIN
KEEP_BOUND = (1677722 << 8) + INT_MIN
COLUMNS = 1024
LINK_FLIPS = (1, 3, 4)
SIZES = (144, 112)
BEGINS = (0, 144)
THIRDS = (
    ((0, 48, (0, 3, 6, 8)), (48, 48, (0, 3, 5, 8)), (96, 48, (0, 2, 5, 8))),
    ((0, 48, (0, 3, 6, 8)), (48, 32, (0, 3, 5, 8)), (80, 32, (0, 2, 5, 8))),
)
SET_LINKS = ((0, 1, 2), (1, 2, 0), (2, 0, 1))
MIB = 1 << 20
LANES = 128


def units(s, parts):
    found, offset = [], 0
    for part in parts:
        for row, count, cuts in THIRDS[part]:
            for unit in range(cuts[s], cuts[s + 1]):
                found.append((BEGINS[part] + row, count, unit, offset))
                offset += count
    return found, offset


def xor_shift(value):
    return value ^ lax.shift_right_logical(value, jnp.int32(16))


def mixing(value):
    value = xor_shift(value) * 73244475
    value = xor_shift(value) * 73244475
    return xor_shift(value)


def pack_body(k_hbm, v_hbm, out, k, sems):
    k_copy = pltpu.make_async_copy(k_hbm, k, sems.at[0])
    v_copy = pltpu.make_async_copy(v_hbm, out.at[1], sems.at[1])
    k_copy.start()
    v_copy.start()
    k_copy.wait()
    turned = k[...].T
    out[0, :HD] = turned[:, :128]
    out[0, HD:] = turned[:, 128:]
    v_copy.wait()


def pack(k, v):
    return pl.pallas_call(
        pack_body,
        out_shape=jax.ShapeDtypeStruct((2, ROWS, HD), jnp.bfloat16),
        in_specs=[pl.BlockSpec(memory_space=pltpu.HBM)] * 2,
        out_specs=pl.BlockSpec(memory_space=pltpu.VMEM),
        scratch_shapes=[pltpu.VMEM((ROWS, HD), jnp.bfloat16), pltpu.SemaphoreType.DMA((2,))],
        compiler_params=pltpu.CompilerParams(vmem_limit_bytes=1 * MIB),
        name="pack",
    )(in_hbm(k), in_hbm(v))


def in_hbm(array):
    return pltpu.with_memory_space_constraint(array, pltpu.HBM)


def row_low(starts, row):
    low = jnp.zeros_like(row)
    for v in range(1, 8):
        low = jnp.maximum(low, jnp.where(row >= starts[v], starts[v], 0))
    return low


def slot_flip(slot):
    return (slot & 1) ^ (3 * ((slot >> 1) & 1)) ^ (4 * (slot >> 2))


def prepare_body(seed_ref, docs_hbm, q_hbm, w_hbm, keep, query, weight, starts, docs, q, row_hash, sems):
    ctx = lax.axis_index("ctx")
    tp = lax.axis_index("tp")
    docs_copy = pltpu.make_async_copy(docs_hbm, docs, sems.at[8])
    docs_copy.start()
    q_copy = pltpu.make_async_copy(q_hbm, q, sems.at[9])
    q_copy.start()
    w_copies = []
    for slot in range(8):
        column = pl.multiple_of((tp ^ slot_flip(slot)) * COLUMNS, COLUMNS)
        w_copies.append(
            pltpu.make_async_copy(
                w_hbm.at[:, pl.ds(column, COLUMNS)], weight.at[slot], sems.at[slot]
            )
        )
        w_copies[-1].start()

    row0 = ctx * ROWS
    head0 = tp * GROUP
    seed = seed_ref[0]
    rows = row0 + lax.broadcasted_iota(jnp.int32, (ROWS, 128), 0)
    lanes = lax.broadcasted_iota(jnp.int32, (ROWS, 128), 1)
    for h in range(GROUP):
        head_hash = mixing(jnp.full((8, 128), seed * 7919 + head0 + h, jnp.int32))[:1]
        row_hash[h] = mixing(head_hash ^ (rows * 65537)) + lanes
    docs_copy.wait()
    starts[0] = 0
    for v in range(1, 8):
        starts[v] = jnp.sum((docs[...] < v).astype(jnp.int32))
    n = (row0 - (row_low(starts, row0) & -ROWS)) // ROWS

    def step(t, _):
        for u in range(STEP):
            start = row0 - (STEP * t + u) * ROWS
            used = STEP * t + u <= n

            @pl.when(used)
            def _():
                def head(h, _):
                    for begin, count in zip(BEGINS, SIZES):
                        for half in range(2):
                            value = row_hash[h, begin : begin + count] + (start + half * 128)
                            value = xor_shift(value) * 73244475
                            value = xor_shift(value) * 73244475
                            kept = (value ^ KEEP_FLIP) >= KEEP_BOUND
                            lane = u * ROWS + half * 128
                            place = pl.ds(GROUP * begin + h * count, count)
                            keep[t, place, lane : lane + 128] = jnp.where(
                                kept, jnp.float32(1), jnp.float32(0)
                            ).astype(jnp.bfloat16)
                    return 0

                lax.fori_loop(0, GROUP, head, 0)

            @pl.when(jnp.logical_not(used))
            def _():
                keep[t, :, u * ROWS : (u + 1) * ROWS] = jnp.zeros((GROUP * ROWS, ROWS), jnp.bfloat16)

        return 0

    lax.fori_loop(0, n // STEP + 1, step, 0)
    q_copy.wait()
    for begin, count in zip(BEGINS, SIZES):
        for h in range(GROUP):
            scaled = q[begin : begin + count, h * HD : (h + 1) * HD].astype(jnp.float32) * QUERY_SCALE
            high = scaled.astype(jnp.bfloat16)
            low = (scaled - high.astype(jnp.float32)).astype(jnp.bfloat16)
            place = slice(GROUP * begin + h * count, GROUP * begin + (h + 1) * count)
            query[place, :HD] = high
            query[place, HD:] = low
    for copy in w_copies:
        copy.wait()


def prepare(seed, docs, queries, weight):
    vmem = pl.BlockSpec(memory_space=pltpu.VMEM)
    hbm = pl.BlockSpec(memory_space=pltpu.HBM)
    smem = pl.BlockSpec(memory_space=pltpu.SMEM)
    return pl.pallas_call(
        prepare_body,
        out_shape=[
            jax.ShapeDtypeStruct((STEPS, GROUP * ROWS, STEP * ROWS), jnp.bfloat16),
            jax.ShapeDtypeStruct((GROUP * ROWS, 2 * HD), jnp.bfloat16),
            jax.ShapeDtypeStruct((8, GROUP * HD, COLUMNS), jnp.bfloat16),
            jax.ShapeDtypeStruct((8,), jnp.int32),
        ],
        in_specs=[smem, hbm, hbm, hbm],
        out_specs=[vmem, vmem, vmem, smem],
        scratch_shapes=[
            pltpu.VMEM((32, 128), jnp.int32),
            pltpu.VMEM((ROWS, GROUP * HD), jnp.bfloat16),
            pltpu.VMEM((GROUP, ROWS, 128), jnp.int32),
            pltpu.SemaphoreType.DMA((10,)),
        ],
        compiler_params=pltpu.CompilerParams(vmem_limit_bytes=4 * MIB),
        cost_estimate=pl.CostEstimate(
            flops=400_000_000, bytes_accessed=28 * MIB, transcendentals=0
        ),
        name="prepare",
    )(seed, docs, queries, weight)


def project_body(side, parts, mixed, weight, outs):
    for s, out in enumerate(outs):
        found, _ = units(s, parts)
        low = min(unit for _, _, unit, _ in found)
        high = max(unit for _, _, unit, _ in found) + 1
        for slot in range(8):
            one, two, three = ((slot >> k) & 1 for k in SET_LINKS[s])
            if one != side:
                continue
            product = jnp.dot(
                mixed, weight[slot, :, low * LANES : high * LANES], preferred_element_type=jnp.float32
            ).astype(jnp.bfloat16)
            for row, count, unit, offset in found:
                row, lane = row - BEGINS[parts[0]], (unit - low) * LANES
                out[2 * two + three, offset : offset + count] = product[
                    row : row + count, lane : lane + LANES
                ]


def slots(count, parts):
    return [jax.ShapeDtypeStruct((count, units(s, parts)[1], LANES), jnp.bfloat16) for s in range(3)]


def rest_body(first, second, weight, *outs):
    mixed = jnp.concatenate([first[...], second[...]], axis=0)
    project_body(0, (0, 1), mixed, weight, outs)


def project_rest(first, second, weight):
    vmem = pl.BlockSpec(memory_space=pltpu.VMEM)
    return pl.pallas_call(
        rest_body,
        out_shape=slots(4, (0, 1)),
        in_specs=[vmem] * 3,
        out_specs=[vmem] * 3,
        compiler_params=pltpu.CompilerParams(vmem_limit_bytes=6 * MIB),
        cost_estimate=pl.CostEstimate(
            flops=2_100_000_000, bytes_accessed=4 * MIB, transcendentals=0
        ),
        name="rest",
    )(first, second, weight)


def turn_body(own, other, keys, values):
    core = lax.axis_index("ctx") & 1
    for d in range(BACK + 1):
        t, lane = d // STEP, d % STEP * ROWS
        source, at = (other, (d + 1) // 2 - core) if d % 2 else (own, d // 2)
        for half in range(2):
            turned = source[at, 0, half * HD : (half + 1) * HD]
            at_lane = slice(lane + half * 128, lane + (half + 1) * 128)
            keys[t, :HD, at_lane] = turned
            keys[t, HD:, at_lane] = turned
        values[t, lane : lane + ROWS] = source[at, 1]


def attend_body(part, starts, query, *refs):
    if part:
        keys, values, keep, weight, mixed, *refs = refs
    else:
        own, other, keep, weight, keys, values, mixed, *refs = refs
        turn_body(own, other, keys, values)
    sends = refs[:3]
    score, peak, total, accum, bias = refs[3:]
    block0 = lax.axis_index("ctx") * ROWS
    n = (block0 - (row_low(starts, block0) & -ROWS)) // ROWS
    rows = SIZES[part]
    row0 = block0 + BEGINS[part]
    span = slice(GROUP * BEGINS[part], GROUP * (BEGINS[part] + rows))
    last_low = row_low(starts, row0 + rows - 1)
    peak[...] = jnp.full(peak.shape, -3e38, jnp.float32)
    total[...] = jnp.zeros(total.shape, jnp.float32)
    accum[...] = jnp.zeros(accum.shape, jnp.float32)

    def score_step(t, masked):
        value = jnp.dot(query[span], keys[t], preferred_element_type=jnp.float32)
        if masked:
            lane = lax.broadcasted_iota(jnp.int32, (rows, STEP * ROWS), 1)
            key_pos = block0 - STEP * t * ROWS - (lane & -ROWS) + (lane & (ROWS - 1))
            row_pos = row0 + lax.broadcasted_iota(jnp.int32, (rows, 1), 0)
            allowed = (key_pos >= row_low(starts, row_pos)) & (key_pos <= row_pos)
            bias[...] = jnp.where(allowed, jnp.float32(0), jnp.float32(-1e30))
            value = value.reshape(GROUP, rows, STEP * ROWS) + bias[...][None]
            value = value.reshape(GROUP * rows, STEP * ROWS)
        score[t] = value
        top = peak[...]
        for k in range(STEP * ROWS // 128):
            top = jnp.maximum(top, value[:, k * 128 : (k + 1) * 128])
        peak[...] = top

    def score_loop(t, _):
        free = (t > 0) & (block0 - (STEP * t + STEP - 1) * ROWS >= last_low)

        @pl.when(free)
        def _():
            score_step(t, False)

        @pl.when(jnp.logical_not(free))
        def _():
            score_step(t, True)

        return 0

    lax.fori_loop(0, n // STEP + 1, score_loop, 0)
    peak[...] = jnp.broadcast_to(jnp.max(peak[...], axis=1, keepdims=True), peak.shape)

    def value_loop(t, _):
        top = peak[...]
        added = total[...]
        probs = []
        for k in range(STEP * ROWS // 128):
            prob = jnp.exp2(score[t, :, k * 128 : (k + 1) * 128] - top)
            added = added + prob
            probs.append(prob.astype(jnp.bfloat16))
        total[...] = added
        prob = jnp.concatenate(probs, axis=1) * keep[t, span]
        accum[...] = accum[...] + jnp.dot(prob, values[t], preferred_element_type=jnp.float32)
        return 0

    lax.fori_loop(0, n // STEP + 1, value_loop, 0)
    for h in range(GROUP):
        at = slice(h * rows, (h + 1) * rows)
        row_sum = jnp.sum(total[at], axis=1, keepdims=True) * 0.9
        mixed[:, h * HD : (h + 1) * HD] = (accum[at] / row_sum).astype(jnp.bfloat16)

    project_body(1, (part,), mixed[...], weight, sends)


def attend(part, starts, query, sources, keep, weight):
    vmem = pl.BlockSpec(memory_space=pltpu.VMEM)
    rows = SIZES[part]
    heads_rows = GROUP * rows
    out_shape = [
        jax.ShapeDtypeStruct((STEPS, 2 * HD, STEP * ROWS), jnp.bfloat16),
        jax.ShapeDtypeStruct((STEPS, STEP * ROWS, HD), jnp.bfloat16),
        jax.ShapeDtypeStruct((rows, GROUP * HD), jnp.bfloat16),
    ] + slots(4, (part,))
    out_shape = out_shape[2 if part else 0 :]
    return pl.pallas_call(
        functools.partial(attend_body, part),
        out_shape=out_shape,
        in_specs=[pl.BlockSpec(memory_space=pltpu.SMEM)] + [vmem] * 5,
        out_specs=[vmem] * len(out_shape),
        scratch_shapes=[
            pltpu.VMEM((STEPS, heads_rows, STEP * ROWS), jnp.float32),
            pltpu.VMEM((heads_rows, 128), jnp.float32),
            pltpu.VMEM((heads_rows, 128), jnp.float32),
            pltpu.VMEM((heads_rows, HD), jnp.float32),
            pltpu.VMEM((rows, STEP * ROWS), jnp.float32),
        ],
        compiler_params=pltpu.CompilerParams(vmem_limit_bytes=16 * MIB),
        cost_estimate=pl.CostEstimate(
            flops=3_000_000_000, bytes_accessed=16 * MIB, transcendentals=3_000_000
        ),
        name=f"attend_{part}",
    )(starts, query, *sources, keep, weight)


def fold_body(count, *refs):
    rest, got, (kept, sent) = refs[0], refs[1:-2], refs[-2:]
    offset = 0
    for other in got:
        rows = other.shape[1]
        for j in range(count):
            held = rest[j, offset : offset + rows].astype(jnp.float32) + other[j].astype(jnp.float32)
            target = kept if j < count // 2 else sent
            target[j % (count // 2), offset : offset + rows] = held.astype(jnp.bfloat16)
        offset += rows


def fold(rest, got):
    vmem = pl.BlockSpec(memory_space=pltpu.VMEM)
    count = rest.shape[0]
    half = jax.ShapeDtypeStruct((count // 2,) + rest.shape[1:], jnp.bfloat16)
    return pl.pallas_call(
        functools.partial(fold_body, count),
        out_shape=[half] * 2,
        in_specs=[vmem] * (1 + len(got)),
        out_specs=[vmem] * 2,
        compiler_params=pltpu.CompilerParams(vmem_limit_bytes=2 * MIB),
        cost_estimate=pl.CostEstimate(flops=300_000, bytes_accessed=MIB, transcendentals=0),
        name=f"fold_{count}",
    )(rest, *got)


def finish_body(*refs):
    out = refs[6]
    for s in range(3):
        for row, count, unit, offset in units(s, (0, 1))[0]:
            held = refs[2 * s][0, offset : offset + count].astype(jnp.float32)
            held = held + refs[2 * s + 1][0, offset : offset + count].astype(jnp.float32)
            out[row : row + count, unit * LANES : (unit + 1) * LANES] = held.astype(jnp.bfloat16)


def finish(pairs):
    vmem = pl.BlockSpec(memory_space=pltpu.VMEM)
    return pl.pallas_call(
        finish_body,
        out_shape=jax.ShapeDtypeStruct((ROWS, COLUMNS), jnp.bfloat16),
        in_specs=[vmem] * 6,
        out_specs=vmem,
        compiler_params=pltpu.CompilerParams(vmem_limit_bytes=4 * MIB),
        name="finish",
    )(*pairs)


def swap(array, flip):
    return lax.ppermute(array, "tp", [(i, i ^ flip) for i in range(8)])


def after(first, second):
    return lax.optimization_barrier((first, second))


def body(queries, key_proj, value_proj, out_weight, doc_ids, drop_seed):
    own = pack(key_proj, value_proj)
    column = [own] * 5
    for chips in (2, 4, 1, 3):
        pairs = [(i, (i + 2 * chips) % 16) for i in range(16)]
        column[chips] = lax.ppermute(own, "ctx", pairs)
    column = jnp.stack(column)
    keep, query, weight, starts = prepare(
        drop_seed, in_hbm(doc_ids.reshape(32, 128)), in_hbm(queries), in_hbm(out_weight)
    )
    column, keep = after(column, keep)
    other = lax.ppermute(column, "ctx", [(i, i ^ 1) for i in range(16)])

    keys, values, first, *sent = attend(0, starts, query, (column, other), keep, weight)
    keep, sent = after(keep, sent)
    got = [[swap(sent[s], LINK_FLIPS[SET_LINKS[s][0]])] for s in range(3)]
    second, *sent = attend(1, starts, query, (keys, values), keep, weight)
    second, sent = after(second, sent)
    for s in range(3):
        sent[s], got[s] = after(sent[s], got[s])
        got[s].append(swap(sent[s], LINK_FLIPS[SET_LINKS[s][0]]))
    rest = list(project_rest(first, second, weight))
    order = second
    for step in (1, 2):
        for s in range(3):
            rest[s], got[s], order = lax.optimization_barrier((rest[s], got[s], order))
            rest[s], order = fold(rest[s], got[s])
            got[s] = [swap(order, LINK_FLIPS[SET_LINKS[s][step]])]
    return finish([array for s in range(3) for array in (rest[s], got[s][0])])


def solution(mesh):
    in_specs = (P("ctx", "tp"), P("ctx", "tp"), P("ctx", "tp"), P("tp", None), P(), P())
    return jax.shard_map(
        body, mesh=mesh, in_specs=in_specs, out_specs=P("ctx", "tp"), check_vma=False
    )
```

time: 78.7 us -> 70.4 us (0.89)
  the two profiles are of different devices: /device:TPU:18 before, /device:TPU:20 now
where the time goes in v1:
time: 70.4 us
  Pallas kernels  29.4 us (42%)
  starting transfers between devices  21.1 us (30%)
  waiting for transfers between devices  19 us (27%)
  between operations  0.81 us (1%)
    ppermute x12, waiting for transfers between devices, swap(): return lax.ppermute(array, 'tp', [(i, i ^ flip) for i in range(8)])  17 us
    pallas_call x2, Pallas kernels, attend(): pl.pallas_call(functools.partial(attend_body, part), out_shape=out_shape,...  14.2 us
    ppermute x12, starting transfers between devices, swap(): return lax.ppermute(array, 'tp', [(i, i ^ flip) for i in range(8)])  13.2 us
    pallas_call x1, Pallas kernels, prepare(): pl.pallas_call(prepare_body, out_shape=[jax.ShapeDtypeStruct((STEPS, GROU...  9.1 us
    ppermute x4, starting transfers between devices, body(): column[chips] = lax.ppermute(own, 'ctx', pairs)  7.77 us
    pallas_call x1, Pallas kernels, project_rest(): pl.pallas_call(rest_body, out_shape=slots(4, (0, 1)), in_specs=[vmem] * 3...  3.47 us
    ppermute x1, waiting for transfers between devices, body(): other = lax.ppermute(column, 'ctx', [(i, i ^ 1) for i in range(16)])  2.08 us
  transfers between devices with their start and end apart: 17, of which 7 were waited for; matrix products, arithmetic and copies ran while one was open for 0% of the time, Pallas kernels for 28%

profile of v1, /device:TPU:20, one launch (start us, length us, event | category | flops | bytes accessed | tf_op | source)
XLA Modules:
  0.0 70.4 jit_solution(15139901699240414330)
XLA Ops:
  0.0 0.9 %pack.1 = bf16[2,256,128]{2,1,0:T(8,128)(2,1)S(1)} custom-call(bf16[256,128]{1,0:T(8,128)(2,1)} %k_hbm.1, bf16[256,128]{1,0:T(8,128)(2,1)} %v_hbm.1), custom_call_target="tpu_custom_call" | custom-call | tf_op jit(solution)/shard_map/pack/pallas_call | solution.py:69
  0.9 0.6 collective-permute-start.3
  1.5 2.8 %collective-permute-start.2 = (bf16[2,256,128]{2,1,0:T(8,128)(2,1)S(1)}, bf16[2,256,128]{2,1,0:T(8,128)(2,1)S(1)}, u32[]{:S(2)}, u32[]{:S(2)}) collective-permute-start(bf16[2,256,128]{2,1,0:T(8,128)(2,1)S(1)} %pack.1), channel_id=1, source_target_pairs={{0,48},{8,56},{16,64},{24,72},{32,80},{40,88},{48,96},{56,104},{64... | collective-permute-start | bytes 393224 | tf_op jit(solution)/shard_map/ppermute | solution.py:416
  4.3 1.2 %collective-permute-start.1 = (bf16[2,256,128]{2,1,0:T(8,128)(2,1)S(1)}, bf16[2,256,128]{2,1,0:T(8,128)(2,1)S(1)}, u32[]{:S(2)}, u32[]{:S(2)}) collective-permute-start(bf16[2,256,128]{2,1,0:T(8,128)(2,1)S(1)} %pack.1), channel_id=1, source_target_pairs={{0,32},{8,40},{16,48},{24,56},{32,64},{40,72},{48,80},{56,88},{64,... | collective-permute-start | bytes 393224 | tf_op jit(solution)/shard_map/ppermute | solution.py:416
  5.5 3.2 %collective-permute-start = (bf16[2,256,128]{2,1,0:T(8,128)(2,1)S(1)}, bf16[2,256,128]{2,1,0:T(8,128)(2,1)S(1)}, u32[]{:S(2)}, u32[]{:S(2)}) collective-permute-start(bf16[2,256,128]{2,1,0:T(8,128)(2,1)S(1)} %pack.1), channel_id=1, source_target_pairs={{0,16},{8,24},{16,32},{24,40},{32,48},{40,56},{48,64},{56,72},{64,... | collective-permute-start | bytes 393224 | tf_op jit(solution)/shard_map/ppermute | solution.py:416
  9.4 9.1 %prepare.1 = (bf16[3,2048,768]{2,1,0:T(8,128)(2,1)S(1)}, bf16[2048,256]{1,0:T(8,128)(2,1)S(1)}, bf16[8,1024,1024]{2,1,0:T(8,128)(2,1)S(1)}, s32[8]{0:T(128)S(1)}) custom-call(s32[1]{0:T(128)S(6)} %copy.11.seed_ref, s32[32,128]{1,0:T(8,128)} %bitcast.11, bf16[256,1024]{1,0:T(8,128)(2,1)} %q_hbm.1, bf16[1024,8192]{1,0:T(8,128)(2,1)} %w_hbm.1), custom_call_target="tpu_custom_call" | custom-call | flops 400000000 | bytes 29360128 | tf_op jit(solution)/shard_map/prepare/pallas_call | solution.py:173
  18.7 2.1 %collective-permute-done.4.refs_1_ = bf16[5,2,256,128]{3,2,1,0:T(8,128)(2,1)S(1)} collective-permute-done((bf16[5,2,256,128]{3,2,1,0:T(8,128)(2,1)S(1)}, bf16[5,2,256,128]{3,2,1,0:T(8,128)(2,1)S(1)}, u32[]{:S(2)}, u32[]{:S(2)}) %collective-permute-start.4) | collective-permute-done | bytes 655392 | tf_op jit(solution)/shard_map/ppermute | solution.py:422
  20.8 7.7 %attend_0.1 = (bf16[3,256,768]{2,1,0:T(8,128)(2,1)S(1)}, bf16[3,768,128]{2,1,0:T(8,128)(2,1)S(1)}, bf16[144,1024]{1,0:T(8,128)(2,1)S(1)}, bf16[4,384,128]{2,1,0:...) custom-call(s32[8]{0:T(128)S(1)} %get-tuple-element.61.starts, ...), custom_call_target="tpu_custom_call" | custom-call | flops 3000000000 | bytes 16777216 | tf_op jit(solution)/shard_map/attend_0/pallas_call | solution.py:335
  28.5 2.0 %collective-permute-start.5 = (bf16[4,384,128]{2,1,0:T(8,128)(2,1)S(1)}, bf16[4,384,128]{2,1,0:T(8,128)(2,1)S(1)}, u32[]{:S(2)}, u32[]{:S(2)}) collective-permute-start(bf16[4,384,128]{2,1,0:T(8,128)(2,1)S(1)} %get-tuple-element.77), channel_id=1, source_target_pairs={{0,1},{1,0},{2,3},{3,2},{4,5},{5,4},{6,7},{7,6},{8,9},{9,8},{10,11... | collective-permute-start | bytes 1179656 | tf_op jit(solution)/shard_map/ppermute | solution.py:404
  30.5 2.5 %collective-permute-start.10 = (bf16[4,384,128]{2,1,0:T(8,128)(2,1)S(1)}, bf16[4,384,128]{2,1,0:T(8,128)(2,1)S(1)}, u32[]{:S(2)}, u32[]{:S(2)}) collective-permute-start(bf16[4,384,128]{2,1,0:T(8,128)(2,1)S(1)} %get-tuple-element.92), channel_id=1, source_target_pairs={{0,3},{1,2},{2,1},{3,0},{4,7},{5,6},{6,5},{7,4},{8,11},{9,10},{10,... | collective-permute-start | bytes 1179656 | tf_op jit(solution)/shard_map/ppermute | solution.py:404
  33.1 1.3 %collective-permute-start.8 = (bf16[4,384,128]{2,1,0:T(8,128)(2,1)S(1)}, bf16[4,384,128]{2,1,0:T(8,128)(2,1)S(1)}, u32[]{:S(2)}, u32[]{:S(2)}) collective-permute-start(bf16[4,384,128]{2,1,0:T(8,128)(2,1)S(1)} %get-tuple-element.87), channel_id=1, source_target_pairs={{0,4},{1,5},{2,6},{3,7},{4,0},{5,1},{6,2},{7,3},{8,12},{9,13},{10,... | collective-permute-start | bytes 1179656 | tf_op jit(solution)/shard_map/ppermute | solution.py:404
  34.3 6.5 %attend_1.1 = (bf16[112,1024]{1,0:T(8,128)(2,1)S(1)}, bf16[4,304,128]{2,1,0:T(8,128)(2,1)S(1)}, bf16[4,304,128]{2,1,0:T(8,128)(2,1)S(1)}, bf16[4,288,128]{2,1,0:T(8,128)(2,1)S(1)}) custom-call(s32[8]{0:T(128)S(1)} %get-tuple-element.61.starts, bf16[2048,256]{1,0:T(8,128)(2,1)S(1)} %get-tuple-element.62.query, ...), custom_call_target="tpu_custom_call" | custom-call | flops 3000000000 | bytes 16777216 | tf_op jit(solution)/shard_map/attend_1/pallas_call | solution.py:335
  40.8 1.1 %collective-permute-start.6 = (bf16[4,304,128]{2,1,0:T(8,128)(2,1)S(1)}, bf16[4,304,128]{2,1,0:T(8,128)(2,1)S(1)}, u32[]{:S(2)}, u32[]{:S(2)}) collective-permute-start(bf16[4,304,128]{2,1,0:T(8,128)(2,1)S(1)} %get-tuple-element.79), channel_id=1, source_target_pairs={{0,1},{1,0},{2,3},{3,2},{4,5},{5,4},{6,7},{7,6},{8,9},{9,8},{10,11... | collective-permute-start | bytes 933896 | tf_op jit(solution)/shard_map/ppermute | solution.py:404
  41.9 0.6 collective-permute-start.11
  42.5 1.1 %collective-permute-start.9 = (bf16[4,288,128]{2,1,0:T(8,128)(2,1)S(1)}, bf16[4,288,128]{2,1,0:T(8,128)(2,1)S(1)}, u32[]{:S(2)}, u32[]{:S(2)}) collective-permute-start(bf16[4,288,128]{2,1,0:T(8,128)(2,1)S(1)} %get-tuple-element.89), channel_id=1, source_target_pairs={{0,4},{1,5},{2,6},{3,7},{4,0},{5,1},{6,2},{7,3},{8,12},{9,13},{10,... | collective-permute-start | bytes 884744 | tf_op jit(solution)/shard_map/ppermute | solution.py:404
  43.6 3.5 %rest.1 = (bf16[4,688,128]{2,1,0:T(8,128)(2,1)S(1)}, bf16[4,688,128]{2,1,0:T(8,128)(2,1)S(1)}, bf16[4,672,128]{2,1,0:T(8,128)(2,1)S(1)}) custom-call(bf16[144,1024]{1,0:T(8,128)(2,1)S(1)} %get-tuple-element.67.first, bf16[112,1024]{1,0:T(8,128)(2,1)S(1)} %get-tuple-element.74.second, bf16[8,1024,1024]{2,1,0:T(8,128)(2,1)S(1)} %get-tuple-element.66.refs_3_.weight), custom_call_target="tpu_custom_call" | custom-call | flops 2100000000 | bytes 4194304 | tf_op jit(solution)/shard_map/rest/pallas_call | solution.py:227
  47.1 0.7 %collective-permute-done.6.refs_2_ = bf16[4,304,128]{2,1,0:T(8,128)(2,1)S(1)} collective-permute-done((bf16[4,304,128]{2,1,0:T(8,128)(2,1)S(1)}, bf16[4,304,128]{2,1,0:T(8,128)(2,1)S(1)}, u32[]{:S(2)}, u32[]{:S(2)}) %collective-permute-start.6) | collective-permute-done | bytes 311328 | tf_op jit(solution)/shard_map/ppermute | solution.py:404
  47.8 0.2 fold_4.3
  48.0 1.6 %collective-permute-start.7 = (bf16[2,688,128]{2,1,0:T(8,128)(2,1)S(1)}, bf16[2,688,128]{2,1,0:T(8,128)(2,1)S(1)}, u32[]{:S(2)}, u32[]{:S(2)}) collective-permute-start(bf16[2,688,128]{2,1,0:T(8,128)(2,1)S(1)} %get-tuple-element.84), channel_id=1, source_target_pairs={{0,3},{1,2},{2,1},{3,0},{4,7},{5,6},{6,5},{7,4},{8,11},{9,10},{10,... | collective-permute-start | bytes 1056776 | tf_op jit(solution)/shard_map/ppermute | solution.py:404
  49.7 3.7 %collective-permute-done.11.refs_2_ = bf16[4,304,128]{2,1,0:T(8,128)(2,1)S(1)} collective-permute-done((bf16[4,304,128]{2,1,0:T(8,128)(2,1)S(1)}, bf16[4,304,128]{2,1,0:T(8,128)(2,1)S(1)}, u32[]{:S(2)}, u32[]{:S(2)}) %collective-permute-start.11) | collective-permute-done | bytes 311328 | tf_op jit(solution)/shard_map/ppermute | solution.py:404
  53.4 0.2 fold_4.4
  53.6 0.8 %collective-permute-start.13 = (bf16[2,688,128]{2,1,0:T(8,128)(2,1)S(1)}, bf16[2,688,128]{2,1,0:T(8,128)(2,1)S(1)}, u32[]{:S(2)}, u32[]{:S(2)}) collective-permute-start(bf16[2,688,128]{2,1,0:T(8,128)(2,1)S(1)} %get-tuple-element.98), channel_id=1, source_target_pairs={{0,4},{1,5},{2,6},{3,7},{4,0},{5,1},{6,2},{7,3},{8,12},{9,13},{10,... | collective-permute-start | bytes 1056776 | tf_op jit(solution)/shard_map/ppermute | solution.py:404
  54.4 0.2 fold_4.5
  54.6 0.1 collective-permute-start.15
  54.7 2.6 %collective-permute-done.7.refs_1_ = bf16[2,688,128]{2,1,0:T(8,128)(2,1)S(1)} collective-permute-done((bf16[2,688,128]{2,1,0:T(8,128)(2,1)S(1)}, bf16[2,688,128]{2,1,0:T(8,128)(2,1)S(1)}, u32[]{:S(2)}, u32[]{:S(2)}) %collective-permute-start.7) | collective-permute-done | bytes 352288 | tf_op jit(solution)/shard_map/ppermute | solution.py:404
  57.4 0.8 %collective-permute-start.12 = (bf16[1,688,128]{2,1,0:T(8,128)(2,1)S(1)}, bf16[1,688,128]{2,1,0:T(8,128)(2,1)S(1)}, u32[]{:S(2)}, u32[]{:S(2)}) collective-permute-start(bf16[1,688,128]{2,1,0:T(8,128)(2,1)S(1)} %get-tuple-element.106), channel_id=1, source_target_pairs={{0,4},{1,5},{2,6},{3,7},{4,0},{5,1},{6,2},{7,3},{8,12},{9,13},{10,... | collective-permute-start | bytes 528392 | tf_op jit(solution)/shard_map/ppermute | solution.py:404
  58.2 4.0 %collective-permute-done.13.refs_1_ = bf16[2,688,128]{2,1,0:T(8,128)(2,1)S(1)} collective-permute-done((bf16[2,688,128]{2,1,0:T(8,128)(2,1)S(1)}, bf16[2,688,128]{2,1,0:T(8,128)(2,1)S(1)}, u32[]{:S(2)}, u32[]{:S(2)}) %collective-permute-start.13) | collective-permute-done | bytes 352288 | tf_op jit(solution)/shard_map/ppermute | solution.py:404
  62.2 0.1 collective-permute-start.14
  62.3 0.4 collective-permute-done.15.refs_1_
  62.8 1.2 %collective-permute-start.16 = (bf16[1,672,128]{2,1,0:T(8,128)(2,1)S(1)}, bf16[1,672,128]{2,1,0:T(8,128)(2,1)S(1)}, u32[]{:S(2)}, u32[]{:S(2)}) collective-permute-start(bf16[1,672,128]{2,1,0:T(8,128)(2,1)S(1)} %get-tuple-element.116), channel_id=1, source_target_pairs={{0,3},{1,2},{2,1},{3,0},{4,7},{5,6},{6,5},{7,4},{8,11},{9,10},{10,... | collective-permute-start | bytes 516104 | tf_op jit(solution)/shard_map/ppermute | solution.py:404
  64.0 5.5 %collective-permute-done.16.refs_5_ = bf16[1,672,128]{2,1,0:T(8,128)(2,1)S(1)} collective-permute-done((bf16[1,672,128]{2,1,0:T(8,128)(2,1)S(1)}, bf16[1,672,128]{2,1,0:T(8,128)(2,1)S(1)}, u32[]{:S(2)}, u32[]{:S(2)}) %collective-permute-start.16) | collective-permute-done | bytes 172064 | tf_op jit(solution)/shard_map/ppermute | solution.py:404
  69.5 0.9 %finish.1 = bf16[256,1024]{1,0:T(8,128)(2,1)} custom-call(bf16[1,688,128]{2,1,0:T(8,128)(2,1)S(1)} %get-tuple-element.105.refs_0_, bf16[1,688,128]{2,1,0:T(8,128)(2,1)S(1)} %collective-permute-done.12.refs_1_, bf16[1,688,128]{2,1,0:T(8,128)(2,1)S(1)} %get-tuple-element.110.refs_2_, bf16[1,688,128]{2,1,0:T(8,128)(2,1)S(1)} %collective-permute-done.14.refs_3_, ...), custom_call_target="tpu_custom_call" | custom-call | tf_op jit(solution)/shard_map/finish/pallas_call | solution.py:393
  (19 shorter events, 0.5 us)
Async XLA Ops:
  0.9 17.7 %collective-permute-start.3 = (bf16[2,256,128]{2,1,0:T(8,128)(2,1)S(1)}, bf16[2,256,128]{2,1,0:T(8,128)(2,1)S(1)}, u32[]{:S(2)}, u32[]{:S(2)}) collective-permute-start(bf16[2,256,128]{2,1,0:T(8,128)(2,1)S(1)} %pack.1), channel_id=1, source_target_pairs={{0,64},{8,72},{16,80},{24,88},{32,96},{40,104},{48,112},{56,120},{... | collective-permute-start | bytes 393224 | tf_op jit(solution)/shard_map/ppermute | solution.py:416
  1.5 17.0 %collective-permute-start.2 = (bf16[2,256,128]{2,1,0:T(8,128)(2,1)S(1)}, bf16[2,256,128]{2,1,0:T(8,128)(2,1)S(1)}, u32[]{:S(2)}, u32[]{:S(2)}) collective-permute-start(bf16[2,256,128]{2,1,0:T(8,128)(2,1)S(1)} %pack.1), channel_id=1, source_target_pairs={{0,48},{8,56},{16,64},{24,72},{32,80},{40,88},{48,96},{56,104},{64... | collective-permute-start | bytes 393224 | tf_op jit(solution)/shard_map/ppermute | solution.py:416
  4.3 14.2 %collective-permute-start.1 = (bf16[2,256,128]{2,1,0:T(8,128)(2,1)S(1)}, bf16[2,256,128]{2,1,0:T(8,128)(2,1)S(1)}, u32[]{:S(2)}, u32[]{:S(2)}) collective-permute-start(bf16[2,256,128]{2,1,0:T(8,128)(2,1)S(1)} %pack.1), channel_id=1, source_target_pairs={{0,32},{8,40},{16,48},{24,56},{32,64},{40,72},{48,80},{56,88},{64,... | collective-permute-start | bytes 393224 | tf_op jit(solution)/shard_map/ppermute | solution.py:416
  5.5 13.0 %collective-permute-start = (bf16[2,256,128]{2,1,0:T(8,128)(2,1)S(1)}, bf16[2,256,128]{2,1,0:T(8,128)(2,1)S(1)}, u32[]{:S(2)}, u32[]{:S(2)}) collective-permute-start(bf16[2,256,128]{2,1,0:T(8,128)(2,1)S(1)} %pack.1), channel_id=1, source_target_pairs={{0,16},{8,24},{16,32},{24,40},{32,48},{40,56},{48,64},{56,72},{64,... | collective-permute-start | bytes 393224 | tf_op jit(solution)/shard_map/ppermute | solution.py:416
  18.6 2.2 %collective-permute-start.4 = (bf16[5,2,256,128]{3,2,1,0:T(8,128)(2,1)S(1)}, bf16[5,2,256,128]{3,2,1,0:T(8,128)(2,1)S(1)}, u32[]{:S(2)}, u32[]{:S(2)}) collective-permute-start(bf16[5,2,256,128]{3,2,1,0:T(8,128)(2,1)S(1)} %bitcast_dynamic-update-slice_fusion.refs_0_), channel_id=1, source_target_pairs={{0,8},{8,0},{16,24},{24,16},{32,40},{40,32},{48,56},{56,48},{64,72... | collective-permute-start | bytes 1966088 | tf_op jit(solution)/shard_map/ppermute | solution.py:422
  28.5 12.3 %collective-permute-start.5 = (bf16[4,384,128]{2,1,0:T(8,128)(2,1)S(1)}, bf16[4,384,128]{2,1,0:T(8,128)(2,1)S(1)}, u32[]{:S(2)}, u32[]{:S(2)}) collective-permute-start(bf16[4,384,128]{2,1,0:T(8,128)(2,1)S(1)} %get-tuple-element.77), channel_id=1, source_target_pairs={{0,1},{1,0},{2,3},{3,2},{4,5},{5,4},{6,7},{7,6},{8,9},{9,8},{10,11... | collective-permute-start | bytes 1179656 | tf_op jit(solution)/shard_map/ppermute | solution.py:404
  30.5 11.4 %collective-permute-start.10 = (bf16[4,384,128]{2,1,0:T(8,128)(2,1)S(1)}, bf16[4,384,128]{2,1,0:T(8,128)(2,1)S(1)}, u32[]{:S(2)}, u32[]{:S(2)}) collective-permute-start(bf16[4,384,128]{2,1,0:T(8,128)(2,1)S(1)} %get-tuple-element.92), channel_id=1, source_target_pairs={{0,3},{1,2},{2,1},{3,0},{4,7},{5,6},{6,5},{7,4},{8,11},{9,10},{10,... | collective-permute-start | bytes 1179656 | tf_op jit(solution)/shard_map/ppermute | solution.py:404
  33.1 9.5 %collective-permute-start.8 = (bf16[4,384,128]{2,1,0:T(8,128)(2,1)S(1)}, bf16[4,384,128]{2,1,0:T(8,128)(2,1)S(1)}, u32[]{:S(2)}, u32[]{:S(2)}) collective-permute-start(bf16[4,384,128]{2,1,0:T(8,128)(2,1)S(1)} %get-tuple-element.87), channel_id=1, source_target_pairs={{0,4},{1,5},{2,6},{3,7},{4,0},{5,1},{6,2},{7,3},{8,12},{9,13},{10,... | collective-permute-start | bytes 1179656 | tf_op jit(solution)/shard_map/ppermute | solution.py:404
  40.8 7.0 %collective-permute-start.6 = (bf16[4,304,128]{2,1,0:T(8,128)(2,1)S(1)}, bf16[4,304,128]{2,1,0:T(8,128)(2,1)S(1)}, u32[]{:S(2)}, u32[]{:S(2)}) collective-permute-start(bf16[4,304,128]{2,1,0:T(8,128)(2,1)S(1)} %get-tuple-element.79), channel_id=1, source_target_pairs={{0,1},{1,0},{2,3},{3,2},{4,5},{5,4},{6,7},{7,6},{8,9},{9,8},{10,11... | collective-permute-start | bytes 933896 | tf_op jit(solution)/shard_map/ppermute | solution.py:404
  41.9 11.4 %collective-permute-start.11 = (bf16[4,304,128]{2,1,0:T(8,128)(2,1)S(1)}, bf16[4,304,128]{2,1,0:T(8,128)(2,1)S(1)}, u32[]{:S(2)}, u32[]{:S(2)}) collective-permute-start(bf16[4,304,128]{2,1,0:T(8,128)(2,1)S(1)} %get-tuple-element.94), channel_id=1, source_target_pairs={{0,3},{1,2},{2,1},{3,0},{4,7},{5,6},{6,5},{7,4},{8,11},{9,10},{10,... | collective-permute-start | bytes 933896 | tf_op jit(solution)/shard_map/ppermute | solution.py:404
  42.5 11.8 %collective-permute-start.9 = (bf16[4,288,128]{2,1,0:T(8,128)(2,1)S(1)}, bf16[4,288,128]{2,1,0:T(8,128)(2,1)S(1)}, u32[]{:S(2)}, u32[]{:S(2)}) collective-permute-start(bf16[4,288,128]{2,1,0:T(8,128)(2,1)S(1)} %get-tuple-element.89), channel_id=1, source_target_pairs={{0,4},{1,5},{2,6},{3,7},{4,0},{5,1},{6,2},{7,3},{8,12},{9,13},{10,... | collective-permute-start | bytes 884744 | tf_op jit(solution)/shard_map/ppermute | solution.py:404
  48.0 9.3 %collective-permute-start.7 = (bf16[2,688,128]{2,1,0:T(8,128)(2,1)S(1)}, bf16[2,688,128]{2,1,0:T(8,128)(2,1)S(1)}, u32[]{:S(2)}, u32[]{:S(2)}) collective-permute-start(bf16[2,688,128]{2,1,0:T(8,128)(2,1)S(1)} %get-tuple-element.84), channel_id=1, source_target_pairs={{0,3},{1,2},{2,1},{3,0},{4,7},{5,6},{6,5},{7,4},{8,11},{9,10},{10,... | collective-permute-start | bytes 1056776 | tf_op jit(solution)/shard_map/ppermute | solution.py:404
  53.6 8.6 %collective-permute-start.13 = (bf16[2,688,128]{2,1,0:T(8,128)(2,1)S(1)}, bf16[2,688,128]{2,1,0:T(8,128)(2,1)S(1)}, u32[]{:S(2)}, u32[]{:S(2)}) collective-permute-start(bf16[2,688,128]{2,1,0:T(8,128)(2,1)S(1)} %get-tuple-element.98), channel_id=1, source_target_pairs={{0,4},{1,5},{2,6},{3,7},{4,0},{5,1},{6,2},{7,3},{8,12},{9,13},{10,... | collective-permute-start | bytes 1056776 | tf_op jit(solution)/shard_map/ppermute | solution.py:404
  54.6 8.2 %collective-permute-start.15 = (bf16[2,672,128]{2,1,0:T(8,128)(2,1)S(1)}, bf16[2,672,128]{2,1,0:T(8,128)(2,1)S(1)}, u32[]{:S(2)}, u32[]{:S(2)}) collective-permute-start(bf16[2,672,128]{2,1,0:T(8,128)(2,1)S(1)} %get-tuple-element.102), channel_id=1, source_target_pairs={{0,1},{1,0},{2,3},{3,2},{4,5},{5,4},{6,7},{7,6},{8,9},{9,8},{10,11... | collective-permute-start | bytes 1032200 | tf_op jit(solution)/shard_map/ppermute | solution.py:404
  57.4 12.1 %collective-permute-start.12 = (bf16[1,688,128]{2,1,0:T(8,128)(2,1)S(1)}, bf16[1,688,128]{2,1,0:T(8,128)(2,1)S(1)}, u32[]{:S(2)}, u32[]{:S(2)}) collective-permute-start(bf16[1,688,128]{2,1,0:T(8,128)(2,1)S(1)} %get-tuple-element.106), channel_id=1, source_target_pairs={{0,4},{1,5},{2,6},{3,7},{4,0},{5,1},{6,2},{7,3},{8,12},{9,13},{10,... | collective-permute-start | bytes 528392 | tf_op jit(solution)/shard_map/ppermute | solution.py:404
  62.2 7.3 %collective-permute-start.14 = (bf16[1,688,128]{2,1,0:T(8,128)(2,1)S(1)}, bf16[1,688,128]{2,1,0:T(8,128)(2,1)S(1)}, u32[]{:S(2)}, u32[]{:S(2)}) collective-permute-start(bf16[1,688,128]{2,1,0:T(8,128)(2,1)S(1)} %get-tuple-element.111), channel_id=1, source_target_pairs={{0,1},{1,0},{2,3},{3,2},{4,5},{5,4},{6,7},{7,6},{8,9},{9,8},{10,11... | collective-permute-start | bytes 528392 | tf_op jit(solution)/shard_map/ppermute | solution.py:404
  62.8 6.7 %collective-permute-start.16 = (bf16[1,672,128]{2,1,0:T(8,128)(2,1)S(1)}, bf16[1,672,128]{2,1,0:T(8,128)(2,1)S(1)}, u32[]{:S(2)}, u32[]{:S(2)}) collective-permute-start(bf16[1,672,128]{2,1,0:T(8,128)(2,1)S(1)} %get-tuple-element.116), channel_id=1, source_target_pairs={{0,3},{1,2},{2,1},{3,0},{4,7},{5,6},{6,5},{7,4},{8,11},{9,10},{10,... | collective-permute-start | bytes 516104 | tf_op jit(solution)/shard_map/ppermute | solution.py:404

commit v2 on v1

--- a/solution.py
+++ b/solution.py
@@ -28,7 +28,7 @@
     ((0, 48, (0, 3, 6, 8)), (48, 48, (0, 3, 5, 8)), (96, 48, (0, 2, 5, 8))),
     ((0, 48, (0, 3, 6, 8)), (48, 32, (0, 3, 5, 8)), (80, 32, (0, 2, 5, 8))),
 )
-SET_LINKS = ((0, 1, 2), (1, 2, 0), (2, 0, 1))
+SET_LINKS = ((0, 2, 1), (2, 1, 0), (1, 0, 2))
 MIB = 1 << 20
 LANES = 128
 
@@ -195,20 +195,22 @@
 
 
 def project_body(side, parts, mixed, weight, outs):
-    for s, out in enumerate(outs):
-        found, _ = units(s, parts)
-        low = min(unit for _, _, unit, _ in found)
-        high = max(unit for _, _, unit, _ in found) + 1
-        for slot in range(8):
-            one, two, three = ((slot >> k) & 1 for k in SET_LINKS[s])
-            if one != side:
-                continue
-            product = jnp.dot(
-                mixed, weight[slot, :, low * LANES : high * LANES], preferred_element_type=jnp.float32
-            ).astype(jnp.bfloat16)
-            for row, count, unit, offset in found:
+    placed = [units(s, parts)[0] for s in range(3)]
+    for slot in range(8):
+        bits = [[(slot >> k) & 1 for k in SET_LINKS[s]] for s in range(3)]
+        sets = [s for s in range(3) if bits[s][0] == side]
+        if not sets:
+            continue
+        columns = [unit for s in sets for _, _, unit, _ in placed[s]]
+        low, high = min(columns), max(columns) + 1
+        product = jnp.dot(
+            mixed, weight[slot, :, low * LANES : high * LANES], preferred_element_type=jnp.float32
+        ).astype(jnp.bfloat16)
+        for s in sets:
+            at = 2 * bits[s][1] + bits[s][2]
+            for row, count, unit, offset in placed[s]:
                 row, lane = row - BEGINS[parts[0]], (unit - low) * LANES
-                out[2 * two + three, offset : offset + count] = product[
+                outs[s][at, offset : offset + count] = product[
                     row : row + count, lane : lane + LANES
                 ]
 
@@ -237,9 +239,10 @@
     )(first, second, weight)
 
 
-def turn_body(own, other, keys, values):
+def turn_body(n, own, other, keys, values):
     core = lax.axis_index("ctx") & 1
-    for d in range(BACK + 1):
+
+    def place(d):
         t, lane = d // STEP, d % STEP * ROWS
         source, at = (other, (d + 1) // 2 - core) if d % 2 else (own, d // 2)
         for half in range(2):
@@ -249,17 +252,25 @@
             keys[t, HD:, at_lane] = turned
         values[t, lane : lane + ROWS] = source[at, 1]
 
+    for t in range(STEPS):
+
+        @pl.when(STEP * t <= n)
+        def _():
+            for d in range(STEP * t, STEP * (t + 1)):
+                place(d)
+
 
 def attend_body(part, starts, query, *refs):
     if part:
         keys, values, keep, weight, mixed, *refs = refs
     else:
         own, other, keep, weight, keys, values, mixed, *refs = refs
-        turn_body(own, other, keys, values)
     sends = refs[:3]
     score, peak, total, accum, bias = refs[3:]
     block0 = lax.axis_index("ctx") * ROWS
     n = (block0 - (row_low(starts, block0) & -ROWS)) // ROWS
+    if not part:
+        turn_body(n, own, other, keys, values)
     rows = SIZES[part]
     row0 = block0 + BEGINS[part]
     span = slice(GROUP * BEGINS[part], GROUP * (BEGINS[part] + rows))

time: 70.4 us -> 68.5 us (0.973)
  the two profiles are of different devices: /device:TPU:20 before, /device:TPU:18 now
where the time goes in v2:
time: 68.5 us; the launch traced here: 67.2 us
  starting transfers between devices  30.1 us (44%)
  Pallas kernels  20.4 us (30%)
  waiting for transfers between devices  15.8 us (23%)
  between operations  0.81 us (1%)
    ppermute x12, starting transfers between devices, swap(): return lax.ppermute(array, 'tp', [(i, i ^ flip) for i in range(8)])  21.4 us
    ppermute x12, waiting for transfers between devices, swap(): return lax.ppermute(array, 'tp', [(i, i ^ flip) for i in range(8)])  13.7 us
    ppermute x4, starting transfers between devices, body(): column[chips] = lax.ppermute(own, 'ctx', pairs)  8.67 us
    pallas_call x2, Pallas kernels, attend(): pl.pallas_call(functools.partial(attend_body, part), out_shape=out_shape,...  8.01 us
    pallas_call x1, Pallas kernels, prepare(): pl.pallas_call(prepare_body, out_shape=[jax.ShapeDtypeStruct((STEPS, GROU...  6.78 us
    pallas_call x1, Pallas kernels, project_rest(): pl.pallas_call(rest_body, out_shape=slots(4, (0, 1)), in_specs=[vmem] * 3...  2.91 us
    ppermute x1, waiting for transfers between devices, body(): other = lax.ppermute(column, 'ctx', [(i, i ^ 1) for i in range(16)])  2.08 us
  transfers between devices with their start and end apart: 17, of which 8 were waited for; matrix products, arithmetic and copies ran while one was open for 0% of the time, Pallas kernels for 21%

profile of v2, /device:TPU:18, one launch (start us, length us, event | category | flops | bytes accessed | tf_op | source)
XLA Modules:
  0.0 67.2 jit_solution(1535667624305499558)
XLA Ops:
  0.0 0.9 %pack.1 = bf16[2,256,128]{2,1,0:T(8,128)(2,1)S(1)} custom-call(bf16[256,128]{1,0:T(8,128)(2,1)} %k_hbm.1, bf16[256,128]{1,0:T(8,128)(2,1)} %v_hbm.1), custom_call_target="tpu_custom_call" | custom-call | tf_op jit(solution)/shard_map/pack/pallas_call | solution.py:69
  0.9 2.2 %collective-permute-start.3 = (bf16[2,256,128]{2,1,0:T(8,128)(2,1)S(1)}, bf16[2,256,128]{2,1,0:T(8,128)(2,1)S(1)}, u32[]{:S(2)}, u32[]{:S(2)}) collective-permute-start(bf16[2,256,128]{2,1,0:T(8,128)(2,1)S(1)} %pack.1), channel_id=1, source_target_pairs={{0,64},{8,72},{16,80},{24,88},{32,96},{40,104},{48,112},{56,120},{... | collective-permute-start | bytes 393224 | tf_op jit(solution)/shard_map/ppermute | solution.py:427
  3.1 1.2 %collective-permute-start.2 = (bf16[2,256,128]{2,1,0:T(8,128)(2,1)S(1)}, bf16[2,256,128]{2,1,0:T(8,128)(2,1)S(1)}, u32[]{:S(2)}, u32[]{:S(2)}) collective-permute-start(bf16[2,256,128]{2,1,0:T(8,128)(2,1)S(1)} %pack.1), channel_id=1, source_target_pairs={{0,48},{8,56},{16,64},{24,72},{32,80},{40,88},{48,96},{56,104},{64... | collective-permute-start | bytes 393224 | tf_op jit(solution)/shard_map/ppermute | solution.py:427
  4.3 1.5 %collective-permute-start.1 = (bf16[2,256,128]{2,1,0:T(8,128)(2,1)S(1)}, bf16[2,256,128]{2,1,0:T(8,128)(2,1)S(1)}, u32[]{:S(2)}, u32[]{:S(2)}) collective-permute-start(bf16[2,256,128]{2,1,0:T(8,128)(2,1)S(1)} %pack.1), channel_id=1, source_target_pairs={{0,32},{8,40},{16,48},{24,56},{32,64},{40,72},{48,80},{56,88},{64,... | collective-permute-start | bytes 393224 | tf_op jit(solution)/shard_map/ppermute | solution.py:427
  5.8 3.8 %collective-permute-start = (bf16[2,256,128]{2,1,0:T(8,128)(2,1)S(1)}, bf16[2,256,128]{2,1,0:T(8,128)(2,1)S(1)}, u32[]{:S(2)}, u32[]{:S(2)}) collective-permute-start(bf16[2,256,128]{2,1,0:T(8,128)(2,1)S(1)} %pack.1), channel_id=1, source_target_pairs={{0,16},{8,24},{16,32},{24,40},{32,48},{40,56},{48,64},{56,72},{64,... | collective-permute-start | bytes 393224 | tf_op jit(solution)/shard_map/ppermute | solution.py:427
  10.3 6.8 %prepare.1 = (bf16[3,2048,768]{2,1,0:T(8,128)(2,1)S(1)}, bf16[2048,256]{1,0:T(8,128)(2,1)S(1)}, bf16[8,1024,1024]{2,1,0:T(8,128)(2,1)S(1)}, s32[8]{0:T(128)S(1)}) custom-call(s32[1]{0:T(128)S(6)} %copy.11.seed_ref, s32[32,128]{1,0:T(8,128)} %bitcast.11, bf16[256,1024]{1,0:T(8,128)(2,1)} %q_hbm.1, bf16[1024,8192]{1,0:T(8,128)(2,1)} %w_hbm.1), custom_call_target="tpu_custom_call" | custom-call | flops 400000000 | bytes 29360128 | tf_op jit(solution)/shard_map/prepare/pallas_call | solution.py:173
  17.3 2.1 %collective-permute-done.4.refs_1_ = bf16[5,2,256,128]{3,2,1,0:T(8,128)(2,1)S(1)} collective-permute-done((bf16[5,2,256,128]{3,2,1,0:T(8,128)(2,1)S(1)}, bf16[5,2,256,128]{3,2,1,0:T(8,128)(2,1)S(1)}, u32[]{:S(2)}, u32[]{:S(2)}) %collective-permute-start.4) | collective-permute-done | bytes 655392 | tf_op jit(solution)/shard_map/ppermute | solution.py:433
  19.4 4.3 %attend_0.1 = (bf16[3,256,768]{2,1,0:T(8,128)(2,1)S(1)}, bf16[3,768,128]{2,1,0:T(8,128)(2,1)S(1)}, bf16[144,1024]{1,0:T(8,128)(2,1)S(1)}, bf16[4,384,128]{2,1,0:...) custom-call(s32[8]{0:T(128)S(1)} %get-tuple-element.61.starts, ...), custom_call_target="tpu_custom_call" | custom-call | flops 3000000000 | bytes 16777216 | tf_op jit(solution)/shard_map/attend_0/pallas_call | solution.py:346
  23.7 2.0 %collective-permute-start.5 = (bf16[4,384,128]{2,1,0:T(8,128)(2,1)S(1)}, bf16[4,384,128]{2,1,0:T(8,128)(2,1)S(1)}, u32[]{:S(2)}, u32[]{:S(2)}) collective-permute-start(bf16[4,384,128]{2,1,0:T(8,128)(2,1)S(1)} %get-tuple-element.77), channel_id=1, source_target_pairs={{0,1},{1,0},{2,3},{3,2},{4,5},{5,4},{6,7},{7,6},{8,9},{9,8},{10,11... | collective-permute-start | bytes 1179656 | tf_op jit(solution)/shard_map/ppermute | solution.py:415
  25.7 1.3 %collective-permute-start.10 = (bf16[4,384,128]{2,1,0:T(8,128)(2,1)S(1)}, bf16[4,384,128]{2,1,0:T(8,128)(2,1)S(1)}, u32[]{:S(2)}, u32[]{:S(2)}) collective-permute-start(bf16[4,384,128]{2,1,0:T(8,128)(2,1)S(1)} %get-tuple-element.92), channel_id=1, source_target_pairs={{0,4},{1,5},{2,6},{3,7},{4,0},{5,1},{6,2},{7,3},{8,12},{9,13},{10,... | collective-permute-start | bytes 1179656 | tf_op jit(solution)/shard_map/ppermute | solution.py:415
  27.0 2.5 %collective-permute-start.8 = (bf16[4,384,128]{2,1,0:T(8,128)(2,1)S(1)}, bf16[4,384,128]{2,1,0:T(8,128)(2,1)S(1)}, u32[]{:S(2)}, u32[]{:S(2)}) collective-permute-start(bf16[4,384,128]{2,1,0:T(8,128)(2,1)S(1)} %get-tuple-element.87), channel_id=1, source_target_pairs={{0,3},{1,2},{2,1},{3,0},{4,7},{5,6},{6,5},{7,4},{8,11},{9,10},{10,... | collective-permute-start | bytes 1179656 | tf_op jit(solution)/shard_map/ppermute | solution.py:415
  29.5 3.7 %attend_1.1 = (bf16[112,1024]{1,0:T(8,128)(2,1)S(1)}, bf16[4,304,128]{2,1,0:T(8,128)(2,1)S(1)}, bf16[4,304,128]{2,1,0:T(8,128)(2,1)S(1)}, bf16[4,288,128]{2,1,0:T(8,128)(2,1)S(1)}) custom-call(s32[8]{0:T(128)S(1)} %get-tuple-element.61.starts, bf16[2048,256]{1,0:T(8,128)(2,1)S(1)} %get-tuple-element.62.query, ...), custom_call_target="tpu_custom_call" | custom-call | flops 3000000000 | bytes 16777216 | tf_op jit(solution)/shard_map/attend_1/pallas_call | solution.py:346
  33.2 1.7 %collective-permute-done.5.refs_1_ = bf16[4,384,128]{2,1,0:T(8,128)(2,1)S(1)} collective-permute-done((bf16[4,384,128]{2,1,0:T(8,128)(2,1)S(1)}, bf16[4,384,128]{2,1,0:T(8,128)(2,1)S(1)}, u32[]{:S(2)}, u32[]{:S(2)}) %collective-permute-start.5) | collective-permute-done | bytes 393248 | tf_op jit(solution)/shard_map/ppermute | solution.py:415
  34.9 2.1 %collective-permute-start.6 = (bf16[4,304,128]{2,1,0:T(8,128)(2,1)S(1)}, bf16[4,304,128]{2,1,0:T(8,128)(2,1)S(1)}, u32[]{:S(2)}, u32[]{:S(2)}) collective-permute-start(bf16[4,304,128]{2,1,0:T(8,128)(2,1)S(1)} %get-tuple-element.79), channel_id=1, source_target_pairs={{0,1},{1,0},{2,3},{3,2},{4,5},{5,4},{6,7},{7,6},{8,9},{9,8},{10,11... | collective-permute-start | bytes 933896 | tf_op jit(solution)/shard_map/ppermute | solution.py:415
  37.0 0.3 collective-permute-done.10.refs_1_
  37.3 1.3 %collective-permute-start.11 = (bf16[4,304,128]{2,1,0:T(8,128)(2,1)S(1)}, bf16[4,304,128]{2,1,0:T(8,128)(2,1)S(1)}, u32[]{:S(2)}, u32[]{:S(2)}) collective-permute-start(bf16[4,304,128]{2,1,0:T(8,128)(2,1)S(1)} %get-tuple-element.94), channel_id=1, source_target_pairs={{0,4},{1,5},{2,6},{3,7},{4,0},{5,1},{6,2},{7,3},{8,12},{9,13},{10,... | collective-permute-start | bytes 933896 | tf_op jit(solution)/shard_map/ppermute | solution.py:415
  38.6 1.4 %collective-permute-done.8.refs_1_ = bf16[4,384,128]{2,1,0:T(8,128)(2,1)S(1)} collective-permute-done((bf16[4,384,128]{2,1,0:T(8,128)(2,1)S(1)}, bf16[4,384,128]{2,1,0:T(8,128)(2,1)S(1)}, u32[]{:S(2)}, u32[]{:S(2)}) %collective-permute-start.8) | collective-permute-done | bytes 393248 | tf_op jit(solution)/shard_map/ppermute | solution.py:415
  40.0 2.5 %collective-permute-start.9 = (bf16[4,288,128]{2,1,0:T(8,128)(2,1)S(1)}, bf16[4,288,128]{2,1,0:T(8,128)(2,1)S(1)}, u32[]{:S(2)}, u32[]{:S(2)}) collective-permute-start(bf16[4,288,128]{2,1,0:T(8,128)(2,1)S(1)} %get-tuple-element.89), channel_id=1, source_target_pairs={{0,3},{1,2},{2,1},{3,0},{4,7},{5,6},{6,5},{7,4},{8,11},{9,10},{10,... | collective-permute-start | bytes 884744 | tf_op jit(solution)/shard_map/ppermute | solution.py:415
  42.6 2.9 %rest.1 = (bf16[4,688,128]{2,1,0:T(8,128)(2,1)S(1)}, bf16[4,688,128]{2,1,0:T(8,128)(2,1)S(1)}, bf16[4,672,128]{2,1,0:T(8,128)(2,1)S(1)}) custom-call(bf16[144,1024]{1,0:T(8,128)(2,1)S(1)} %get-tuple-element.67.first, bf16[112,1024]{1,0:T(8,128)(2,1)S(1)} %get-tuple-element.74.second, bf16[8,1024,1024]{2,1,0:T(8,128)(2,1)S(1)} %get-tuple-element.66.refs_3_.weight), custom_call_target="tpu_custom_call" | custom-call | flops 2100000000 | bytes 4194304 | tf_op jit(solution)/shard_map/rest/pallas_call | solution.py:229
  45.5 0.2 fold_4.3
  45.7 0.9 %collective-permute-start.7 = (bf16[2,688,128]{2,1,0:T(8,128)(2,1)S(1)}, bf16[2,688,128]{2,1,0:T(8,128)(2,1)S(1)}, u32[]{:S(2)}, u32[]{:S(2)}) collective-permute-start(bf16[2,688,128]{2,1,0:T(8,128)(2,1)S(1)} %get-tuple-element.84), channel_id=1, source_target_pairs={{0,4},{1,5},{2,6},{3,7},{4,0},{5,1},{6,2},{7,3},{8,12},{9,13},{10,... | collective-permute-start | bytes 1056776 | tf_op jit(solution)/shard_map/ppermute | solution.py:415
  46.6 0.5 collective-permute-done.11.refs_2_
  47.1 0.2 fold_4.4
  47.3 3.8 %collective-permute-start.13 = (bf16[2,688,128]{2,1,0:T(8,128)(2,1)S(1)}, bf16[2,688,128]{2,1,0:T(8,128)(2,1)S(1)}, u32[]{:S(2)}, u32[]{:S(2)}) collective-permute-start(bf16[2,688,128]{2,1,0:T(8,128)(2,1)S(1)} %get-tuple-element.98), channel_id=1, source_target_pairs={{0,3},{1,2},{2,1},{3,0},{4,7},{5,6},{6,5},{7,4},{8,11},{9,10},{10,... | collective-permute-start | bytes 1056776 | tf_op jit(solution)/shard_map/ppermute | solution.py:415
  51.0 0.2 fold_4.5
  51.2 0.1 collective-permute-start.15
  51.3 4.4 %collective-permute-done.7.refs_1_ = bf16[2,688,128]{2,1,0:T(8,128)(2,1)S(1)} collective-permute-done((bf16[2,688,128]{2,1,0:T(8,128)(2,1)S(1)}, bf16[2,688,128]{2,1,0:T(8,128)(2,1)S(1)}, u32[]{:S(2)}, u32[]{:S(2)}) %collective-permute-start.7) | collective-permute-done | bytes 352288 | tf_op jit(solution)/shard_map/ppermute | solution.py:415
  55.8 3.9 %collective-permute-start.12 = (bf16[1,688,128]{2,1,0:T(8,128)(2,1)S(1)}, bf16[1,688,128]{2,1,0:T(8,128)(2,1)S(1)}, u32[]{:S(2)}, u32[]{:S(2)}) collective-permute-start(bf16[1,688,128]{2,1,0:T(8,128)(2,1)S(1)} %get-tuple-element.106), channel_id=1, source_target_pairs={{0,3},{1,2},{2,1},{3,0},{4,7},{5,6},{6,5},{7,4},{8,11},{9,10},{10,... | collective-permute-start | bytes 528392 | tf_op jit(solution)/shard_map/ppermute | solution.py:415
  59.9 0.7 %collective-permute-done.15.refs_1_ = bf16[2,672,128]{2,1,0:T(8,128)(2,1)S(1)} collective-permute-done((bf16[2,672,128]{2,1,0:T(8,128)(2,1)S(1)}, bf16[2,672,128]{2,1,0:T(8,128)(2,1)S(1)}, u32[]{:S(2)}, u32[]{:S(2)}) %collective-permute-start.15) | collective-permute-done | bytes 344096 | tf_op jit(solution)/shard_map/ppermute | solution.py:415
  60.7 0.8 %collective-permute-start.16 = (bf16[1,672,128]{2,1,0:T(8,128)(2,1)S(1)}, bf16[1,672,128]{2,1,0:T(8,128)(2,1)S(1)}, u32[]{:S(2)}, u32[]{:S(2)}) collective-permute-start(bf16[1,672,128]{2,1,0:T(8,128)(2,1)S(1)} %get-tuple-element.116), channel_id=1, source_target_pairs={{0,4},{1,5},{2,6},{3,7},{4,0},{5,1},{6,2},{7,3},{8,12},{9,13},{10,... | collective-permute-start | bytes 516104 | tf_op jit(solution)/shard_map/ppermute | solution.py:415
  61.6 4.7 %collective-permute-done.16.refs_5_ = bf16[1,672,128]{2,1,0:T(8,128)(2,1)S(1)} collective-permute-done((bf16[1,672,128]{2,1,0:T(8,128)(2,1)S(1)}, bf16[1,672,128]{2,1,0:T(8,128)(2,1)S(1)}, u32[]{:S(2)}, u32[]{:S(2)}) %collective-permute-start.16) | collective-permute-done | bytes 172064 | tf_op jit(solution)/shard_map/ppermute | solution.py:415
  66.2 0.9 %finish.1 = bf16[256,1024]{1,0:T(8,128)(2,1)} custom-call(bf16[1,688,128]{2,1,0:T(8,128)(2,1)S(1)} %get-tuple-element.105.refs_0_, bf16[1,688,128]{2,1,0:T(8,128)(2,1)S(1)} %collective-permute-done.12.refs_1_, bf16[1,688,128]{2,1,0:T(8,128)(2,1)S(1)} %get-tuple-element.110.refs_2_, bf16[1,688,128]{2,1,0:T(8,128)(2,1)S(1)} %collective-permute-done.14.refs_3_, ...), custom_call_target="tpu_custom_call" | custom-call | tf_op jit(solution)/shard_map/finish/pallas_call | solution.py:404
  (19 shorter events, 0.5 us)
Async XLA Ops:
  0.9 16.2 %collective-permute-start.3 = (bf16[2,256,128]{2,1,0:T(8,128)(2,1)S(1)}, bf16[2,256,128]{2,1,0:T(8,128)(2,1)S(1)}, u32[]{:S(2)}, u32[]{:S(2)}) collective-permute-start(bf16[2,256,128]{2,1,0:T(8,128)(2,1)S(1)} %pack.1), channel_id=1, source_target_pairs={{0,64},{8,72},{16,80},{24,88},{32,96},{40,104},{48,112},{56,120},{... | collective-permute-start | bytes 393224 | tf_op jit(solution)/shard_map/ppermute | solution.py:427
  3.1 14.0 %collective-permute-start.2 = (bf16[2,256,128]{2,1,0:T(8,128)(2,1)S(1)}, bf16[2,256,128]{2,1,0:T(8,128)(2,1)S(1)}, u32[]{:S(2)}, u32[]{:S(2)}) collective-permute-start(bf16[2,256,128]{2,1,0:T(8,128)(2,1)S(1)} %pack.1), channel_id=1, source_target_pairs={{0,48},{8,56},{16,64},{24,72},{32,80},{40,88},{48,96},{56,104},{64... | collective-permute-start | bytes 393224 | tf_op jit(solution)/shard_map/ppermute | solution.py:427
  4.3 12.8 %collective-permute-start.1 = (bf16[2,256,128]{2,1,0:T(8,128)(2,1)S(1)}, bf16[2,256,128]{2,1,0:T(8,128)(2,1)S(1)}, u32[]{:S(2)}, u32[]{:S(2)}) collective-permute-start(bf16[2,256,128]{2,1,0:T(8,128)(2,1)S(1)} %pack.1), channel_id=1, source_target_pairs={{0,32},{8,40},{16,48},{24,56},{32,64},{40,72},{48,80},{56,88},{64,... | collective-permute-start | bytes 393224 | tf_op jit(solution)/shard_map/ppermute | solution.py:427
  5.8 11.3 %collective-permute-start = (bf16[2,256,128]{2,1,0:T(8,128)(2,1)S(1)}, bf16[2,256,128]{2,1,0:T(8,128)(2,1)S(1)}, u32[]{:S(2)}, u32[]{:S(2)}) collective-permute-start(bf16[2,256,128]{2,1,0:T(8,128)(2,1)S(1)} %pack.1), channel_id=1, source_target_pairs={{0,16},{8,24},{16,32},{24,40},{32,48},{40,56},{48,64},{56,72},{64,... | collective-permute-start | bytes 393224 | tf_op jit(solution)/shard_map/ppermute | solution.py:427
  17.2 2.2 %collective-permute-start.4 = (bf16[5,2,256,128]{3,2,1,0:T(8,128)(2,1)S(1)}, bf16[5,2,256,128]{3,2,1,0:T(8,128)(2,1)S(1)}, u32[]{:S(2)}, u32[]{:S(2)}) collective-permute-start(bf16[5,2,256,128]{3,2,1,0:T(8,128)(2,1)S(1)} %bitcast_dynamic-update-slice_fusion.refs_0_), channel_id=1, source_target_pairs={{0,8},{8,0},{16,24},{24,16},{32,40},{40,32},{48,56},{56,48},{64,72... | collective-permute-start | bytes 1966088 | tf_op jit(solution)/shard_map/ppermute | solution.py:433
  23.7 11.1 %collective-permute-start.5 = (bf16[4,384,128]{2,1,0:T(8,128)(2,1)S(1)}, bf16[4,384,128]{2,1,0:T(8,128)(2,1)S(1)}, u32[]{:S(2)}, u32[]{:S(2)}) collective-permute-start(bf16[4,384,128]{2,1,0:T(8,128)(2,1)S(1)} %get-tuple-element.77), channel_id=1, source_target_pairs={{0,1},{1,0},{2,3},{3,2},{4,5},{5,4},{6,7},{7,6},{8,9},{9,8},{10,11... | collective-permute-start | bytes 1179656 | tf_op jit(solution)/shard_map/ppermute | solution.py:415
  25.7 11.6 %collective-permute-start.10 = (bf16[4,384,128]{2,1,0:T(8,128)(2,1)S(1)}, bf16[4,384,128]{2,1,0:T(8,128)(2,1)S(1)}, u32[]{:S(2)}, u32[]{:S(2)}) collective-permute-start(bf16[4,384,128]{2,1,0:T(8,128)(2,1)S(1)} %get-tuple-element.92), channel_id=1, source_target_pairs={{0,4},{1,5},{2,6},{3,7},{4,0},{5,1},{6,2},{7,3},{8,12},{9,13},{10,... | collective-permute-start | bytes 1179656 | tf_op jit(solution)/shard_map/ppermute | solution.py:415
  27.0 13.0 %collective-permute-start.8 = (bf16[4,384,128]{2,1,0:T(8,128)(2,1)S(1)}, bf16[4,384,128]{2,1,0:T(8,128)(2,1)S(1)}, u32[]{:S(2)}, u32[]{:S(2)}) collective-permute-start(bf16[4,384,128]{2,1,0:T(8,128)(2,1)S(1)} %get-tuple-element.87), channel_id=1, source_target_pairs={{0,3},{1,2},{2,1},{3,0},{4,7},{5,6},{6,5},{7,4},{8,11},{9,10},{10,... | collective-permute-start | bytes 1179656 | tf_op jit(solution)/shard_map/ppermute | solution.py:415
  34.9 10.6 %collective-permute-start.6 = (bf16[4,304,128]{2,1,0:T(8,128)(2,1)S(1)}, bf16[4,304,128]{2,1,0:T(8,128)(2,1)S(1)}, u32[]{:S(2)}, u32[]{:S(2)}) collective-permute-start(bf16[4,304,128]{2,1,0:T(8,128)(2,1)S(1)} %get-tuple-element.79), channel_id=1, source_target_pairs={{0,1},{1,0},{2,3},{3,2},{4,5},{5,4},{6,7},{7,6},{8,9},{9,8},{10,11... | collective-permute-start | bytes 933896 | tf_op jit(solution)/shard_map/ppermute | solution.py:415
  37.3 9.8 %collective-permute-start.11 = (bf16[4,304,128]{2,1,0:T(8,128)(2,1)S(1)}, bf16[4,304,128]{2,1,0:T(8,128)(2,1)S(1)}, u32[]{:S(2)}, u32[]{:S(2)}) collective-permute-start(bf16[4,304,128]{2,1,0:T(8,128)(2,1)S(1)} %get-tuple-element.94), channel_id=1, source_target_pairs={{0,4},{1,5},{2,6},{3,7},{4,0},{5,1},{6,2},{7,3},{8,12},{9,13},{10,... | collective-permute-start | bytes 933896 | tf_op jit(solution)/shard_map/ppermute | solution.py:415
  40.0 11.0 %collective-permute-start.9 = (bf16[4,288,128]{2,1,0:T(8,128)(2,1)S(1)}, bf16[4,288,128]{2,1,0:T(8,128)(2,1)S(1)}, u32[]{:S(2)}, u32[]{:S(2)}) collective-permute-start(bf16[4,288,128]{2,1,0:T(8,128)(2,1)S(1)} %get-tuple-element.89), channel_id=1, source_target_pairs={{0,3},{1,2},{2,1},{3,0},{4,7},{5,6},{6,5},{7,4},{8,11},{9,10},{10,... | collective-permute-start | bytes 884744 | tf_op jit(solution)/shard_map/ppermute | solution.py:415
  45.7 10.1 %collective-permute-start.7 = (bf16[2,688,128]{2,1,0:T(8,128)(2,1)S(1)}, bf16[2,688,128]{2,1,0:T(8,128)(2,1)S(1)}, u32[]{:S(2)}, u32[]{:S(2)}) collective-permute-start(bf16[2,688,128]{2,1,0:T(8,128)(2,1)S(1)} %get-tuple-element.84), channel_id=1, source_target_pairs={{0,4},{1,5},{2,6},{3,7},{4,0},{5,1},{6,2},{7,3},{8,12},{9,13},{10,... | collective-permute-start | bytes 1056776 | tf_op jit(solution)/shard_map/ppermute | solution.py:415
  47.3 12.5 %collective-permute-start.13 = (bf16[2,688,128]{2,1,0:T(8,128)(2,1)S(1)}, bf16[2,688,128]{2,1,0:T(8,128)(2,1)S(1)}, u32[]{:S(2)}, u32[]{:S(2)}) collective-permute-start(bf16[2,688,128]{2,1,0:T(8,128)(2,1)S(1)} %get-tuple-element.98), channel_id=1, source_target_pairs={{0,3},{1,2},{2,1},{3,0},{4,7},{5,6},{6,5},{7,4},{8,11},{9,10},{10,... | collective-permute-start | bytes 1056776 | tf_op jit(solution)/shard_map/ppermute | solution.py:415
  51.2 9.4 %collective-permute-start.15 = (bf16[2,672,128]{2,1,0:T(8,128)(2,1)S(1)}, bf16[2,672,128]{2,1,0:T(8,128)(2,1)S(1)}, u32[]{:S(2)}, u32[]{:S(2)}) collective-permute-start(bf16[2,672,128]{2,1,0:T(8,128)(2,1)S(1)} %get-tuple-element.102), channel_id=1, source_target_pairs={{0,1},{1,0},{2,3},{3,2},{4,5},{5,4},{6,7},{7,6},{8,9},{9,8},{10,11... | collective-permute-start | bytes 1032200 | tf_op jit(solution)/shard_map/ppermute | solution.py:415
  55.8 10.4 %collective-permute-start.12 = (bf16[1,688,128]{2,1,0:T(8,128)(2,1)S(1)}, bf16[1,688,128]{2,1,0:T(8,128)(2,1)S(1)}, u32[]{:S(2)}, u32[]{:S(2)}) collective-permute-start(bf16[1,688,128]{2,1,0:T(8,128)(2,1)S(1)} %get-tuple-element.106), channel_id=1, source_target_pairs={{0,3},{1,2},{2,1},{3,0},{4,7},{5,6},{6,5},{7,4},{8,11},{9,10},{10,... | collective-permute-start | bytes 528392 | tf_op jit(solution)/shard_map/ppermute | solution.py:415
  59.8 6.4 %collective-permute-start.14 = (bf16[1,688,128]{2,1,0:T(8,128)(2,1)S(1)}, bf16[1,688,128]{2,1,0:T(8,128)(2,1)S(1)}, u32[]{:S(2)}, u32[]{:S(2)}) collective-permute-start(bf16[1,688,128]{2,1,0:T(8,128)(2,1)S(1)} %get-tuple-element.111), channel_id=1, source_target_pairs={{0,1},{1,0},{2,3},{3,2},{4,5},{5,4},{6,7},{7,6},{8,9},{9,8},{10,11... | collective-permute-start | bytes 528392 | tf_op jit(solution)/shard_map/ppermute | solution.py:415
  60.7 5.5 %collective-permute-start.16 = (bf16[1,672,128]{2,1,0:T(8,128)(2,1)S(1)}, bf16[1,672,128]{2,1,0:T(8,128)(2,1)S(1)}, u32[]{:S(2)}, u32[]{:S(2)}) collective-permute-start(bf16[1,672,128]{2,1,0:T(8,128)(2,1)S(1)} %get-tuple-element.116), channel_id=1, source_target_pairs={{0,4},{1,5},{2,6},{3,7},{4,0},{5,1},{6,2},{7,3},{8,12},{9,13},{10,... | collective-permute-start | bytes 516104 | tf_op jit(solution)/shard_map/ppermute | solution.py:415

commit v3 on v2

--- a/solution.py
+++ b/solution.py
@@ -390,25 +390,48 @@
     )(rest, *got)
 
 
-def finish_body(*refs):
-    out = refs[6]
-    for s in range(3):
-        for row, count, unit, offset in units(s, (0, 1))[0]:
-            held = refs[2 * s][0, offset : offset + count].astype(jnp.float32)
-            held = held + refs[2 * s + 1][0, offset : offset + count].astype(jnp.float32)
-            out[row : row + count, unit * LANES : (unit + 1) * LANES] = held.astype(jnp.bfloat16)
-
-
-def finish(pairs):
+def finish_body(sets, *refs):
+    pairs = refs[: 2 * len(sets)]
+    out, held, sems = refs[-3:]
+    copies = []
+    for part in range(2):
+        for row, count, cuts in THIRDS[part]:
+            row += BEGINS[part]
+            for index, s in enumerate(sets):
+                for place, _, unit, offset in units(s, (0, 1))[0]:
+                    if place != row:
+                        continue
+                    total = pairs[2 * index][0, offset : offset + count].astype(jnp.float32)
+                    total = total + pairs[2 * index + 1][0, offset : offset + count].astype(jnp.float32)
+                    held[row : row + count, unit * LANES : (unit + 1) * LANES] = total.astype(jnp.bfloat16)
+            columns = slice(cuts[sets[0]] * LANES, cuts[sets[-1] + 1] * LANES)
+            copies.append(
+                pltpu.make_async_copy(
+                    held.at[row : row + count, columns],
+                    out.at[row : row + count, columns],
+                    sems.at[len(copies)],
+                )
+            )
+            copies[-1].start()
+    for copy in copies:
+        copy.wait()
+
+
+def finish(sets, pairs, before):
     vmem = pl.BlockSpec(memory_space=pltpu.VMEM)
-    return pl.pallas_call(
-        finish_body,
+    hbm = pl.BlockSpec(memory_space=pltpu.HBM)
+    old = [] if before is None else [before]
+    return pl.pallas_call(
+        functools.partial(finish_body, sets),
         out_shape=jax.ShapeDtypeStruct((ROWS, COLUMNS), jnp.bfloat16),
-        in_specs=[vmem] * 6,
-        out_specs=vmem,
+        in_specs=[vmem] * len(pairs) + [hbm] * len(old),
+        out_specs=hbm,
+        input_output_aliases={len(pairs): 0} if old else {},
+        scratch_shapes=[pltpu.VMEM((ROWS, COLUMNS), jnp.bfloat16), pltpu.SemaphoreType.DMA((6,))],
         compiler_params=pltpu.CompilerParams(vmem_limit_bytes=4 * MIB),
-        name="finish",
-    )(*pairs)
+        cost_estimate=pl.CostEstimate(flops=300_000, bytes_accessed=MIB, transcendentals=0),
+        name=f"finish_{sets[0]}",
+    )(*pairs, *old)
 
 
 def swap(array, flip):
@@ -447,7 +470,9 @@
             rest[s], got[s], order = lax.optimization_barrier((rest[s], got[s], order))
             rest[s], order = fold(rest[s], got[s])
             got[s] = [swap(order, LINK_FLIPS[SET_LINKS[s][step]])]
-    return finish([array for s in range(3) for array in (rest[s], got[s][0])])
+    pairs = [(rest[s], got[s][0]) for s in range(3)]
+    result = finish((0, 1), pairs[0] + pairs[1], None)
+    return finish((2,), pairs[2], result)
 
 
 def solution(mesh):

time: 68.5 us -> 69.8 us (1.019)
  the two profiles are of different devices: /device:TPU:18 before, /device:TPU:6 now
where the time goes in v3:
time: 69.8 us; the launch traced here: 68.9 us
  Pallas kernels  28 us (40%)
  starting transfers between devices  26.8 us (38%)
  waiting for transfers between devices  13 us (19%)
  between operations  0.98 us (1%)
    ppermute x12, starting transfers between devices, swap(): return lax.ppermute(array, 'tp', [(i, i ^ flip) for i in range(8)])  19.7 us
    pallas_call x2, Pallas kernels, attend(): pl.pallas_call(functools.partial(attend_body, part), out_shape=out_shape,...  13.5 us
    ppermute x12, waiting for transfers between devices, swap(): return lax.ppermute(array, 'tp', [(i, i ^ flip) for i in range(8)])  10.9 us
    pallas_call x1, Pallas kernels, prepare(): pl.pallas_call(prepare_body, out_shape=[jax.ShapeDtypeStruct((STEPS, GROU...  8.37 us
    ppermute x4, starting transfers between devices, body(): column[chips] = lax.ppermute(own, 'ctx', pairs)  6.97 us
    pallas_call x1, Pallas kernels, project_rest(): pl.pallas_call(rest_body, out_shape=slots(4, (0, 1)), in_specs=[vmem] * 3...  2.91 us
    ppermute x1, waiting for transfers between devices, body(): other = lax.ppermute(column, 'ctx', [(i, i ^ 1) for i in range(16)])  2.08 us
    pallas_call x2, Pallas kernels, finish(): pl.pallas_call(functools.partial(finish_body, sets), out_shape=jax.ShapeD...  1.51 us
  transfers between devices with their start and end apart: 17, of which 7 were waited for; matrix products, arithmetic and copies ran while one was open for 0% of the time, Pallas kernels for 28%

profile of v3, /device:TPU:6, one launch (start us, length us, event | category | flops | bytes accessed | tf_op | source)
XLA Modules:
  0.0 68.9 jit_solution(8045647851334937239)
XLA Ops:
  0.0 0.9 %pack.1 = bf16[2,256,128]{2,1,0:T(8,128)(2,1)S(1)} custom-call(bf16[256,128]{1,0:T(8,128)(2,1)} %k_hbm.1, bf16[256,128]{1,0:T(8,128)(2,1)} %v_hbm.1), custom_call_target="tpu_custom_call" | custom-call | tf_op jit(solution)/shard_map/pack/pallas_call | solution.py:69
  0.9 1.5 %collective-permute-start.3 = (bf16[2,256,128]{2,1,0:T(8,128)(2,1)S(1)}, bf16[2,256,128]{2,1,0:T(8,128)(2,1)S(1)}, u32[]{:S(2)}, u32[]{:S(2)}) collective-permute-start(bf16[2,256,128]{2,1,0:T(8,128)(2,1)S(1)} %pack.1), channel_id=1, source_target_pairs={{0,64},{8,72},{16,80},{24,88},{32,96},{40,104},{48,112},{56,120},{... | collective-permute-start | bytes 393224 | tf_op jit(solution)/shard_map/ppermute | solution.py:450
  2.4 4.7 %collective-permute-start.2 = (bf16[2,256,128]{2,1,0:T(8,128)(2,1)S(1)}, bf16[2,256,128]{2,1,0:T(8,128)(2,1)S(1)}, u32[]{:S(2)}, u32[]{:S(2)}) collective-permute-start(bf16[2,256,128]{2,1,0:T(8,128)(2,1)S(1)} %pack.1), channel_id=1, source_target_pairs={{0,48},{8,56},{16,64},{24,72},{32,80},{40,88},{48,96},{56,104},{64... | collective-permute-start | bytes 393224 | tf_op jit(solution)/shard_map/ppermute | solution.py:450
  7.1 0.6 collective-permute-start.1
  7.7 0.2 collective-permute-start
  8.6 8.4 %prepare.1 = (bf16[3,2048,768]{2,1,0:T(8,128)(2,1)S(1)}, bf16[2048,256]{1,0:T(8,128)(2,1)S(1)}, bf16[8,1024,1024]{2,1,0:T(8,128)(2,1)S(1)}, s32[8]{0:T(128)S(1)}) custom-call(s32[1]{0:T(128)S(6)} %copy.13.seed_ref, s32[32,128]{1,0:T(8,128)} %bitcast.11, bf16[256,1024]{1,0:T(8,128)(2,1)} %q_hbm.1, bf16[1024,8192]{1,0:T(8,128)(2,1)} %w_hbm.1), custom_call_target="tpu_custom_call" | custom-call | flops 400000000 | bytes 29360128 | tf_op jit(solution)/shard_map/prepare/pallas_call | solution.py:173
  17.2 2.1 %collective-permute-done.4.refs_1_ = bf16[5,2,256,128]{3,2,1,0:T(8,128)(2,1)S(1)} collective-permute-done((bf16[5,2,256,128]{3,2,1,0:T(8,128)(2,1)S(1)}, bf16[5,2,256,128]{3,2,1,0:T(8,128)(2,1)S(1)}, u32[]{:S(2)}, u32[]{:S(2)}) %collective-permute-start.4) | collective-permute-done | bytes 655392 | tf_op jit(solution)/shard_map/ppermute | solution.py:456
  19.3 7.4 %attend_0.1 = (bf16[3,256,768]{2,1,0:T(8,128)(2,1)S(1)}, bf16[3,768,128]{2,1,0:T(8,128)(2,1)S(1)}, bf16[144,1024]{1,0:T(8,128)(2,1)S(1)}, bf16[4,384,128]{2,1,0:...) custom-call(s32[8]{0:T(128)S(1)} %get-tuple-element.61.starts, ...), custom_call_target="tpu_custom_call" | custom-call | flops 3000000000 | bytes 16777216 | tf_op jit(solution)/shard_map/attend_0/pallas_call | solution.py:346
  26.7 2.1 %collective-permute-start.9 = (bf16[4,384,128]{2,1,0:T(8,128)(2,1)S(1)}, bf16[4,384,128]{2,1,0:T(8,128)(2,1)S(1)}, u32[]{:S(2)}, u32[]{:S(2)}) collective-permute-start(bf16[4,384,128]{2,1,0:T(8,128)(2,1)S(1)} %get-tuple-element.87), channel_id=1, source_target_pairs={{0,1},{1,0},{2,3},{3,2},{4,5},{5,4},{6,7},{7,6},{8,9},{9,8},{10,11... | collective-permute-start | bytes 1179656 | tf_op jit(solution)/shard_map/ppermute | solution.py:438
  28.8 1.6 %collective-permute-start.7 = (bf16[4,384,128]{2,1,0:T(8,128)(2,1)S(1)}, bf16[4,384,128]{2,1,0:T(8,128)(2,1)S(1)}, u32[]{:S(2)}, u32[]{:S(2)}) collective-permute-start(bf16[4,384,128]{2,1,0:T(8,128)(2,1)S(1)} %get-tuple-element.82), channel_id=1, source_target_pairs={{0,4},{1,5},{2,6},{3,7},{4,0},{5,1},{6,2},{7,3},{8,12},{9,13},{10,... | collective-permute-start | bytes 1179656 | tf_op jit(solution)/shard_map/ppermute | solution.py:438
  30.3 2.5 %collective-permute-start.5 = (bf16[4,384,128]{2,1,0:T(8,128)(2,1)S(1)}, bf16[4,384,128]{2,1,0:T(8,128)(2,1)S(1)}, u32[]{:S(2)}, u32[]{:S(2)}) collective-permute-start(bf16[4,384,128]{2,1,0:T(8,128)(2,1)S(1)} %get-tuple-element.77), channel_id=1, source_target_pairs={{0,3},{1,2},{2,1},{3,0},{4,7},{5,6},{6,5},{7,4},{8,11},{9,10},{10,... | collective-permute-start | bytes 1179656 | tf_op jit(solution)/shard_map/ppermute | solution.py:438
  32.8 6.1 %attend_1.1 = (bf16[112,1024]{1,0:T(8,128)(2,1)S(1)}, bf16[4,304,128]{2,1,0:T(8,128)(2,1)S(1)}, bf16[4,304,128]{2,1,0:T(8,128)(2,1)S(1)}, bf16[4,288,128]{2,1,0:T(8,128)(2,1)S(1)}) custom-call(s32[8]{0:T(128)S(1)} %get-tuple-element.61.starts, bf16[2048,256]{1,0:T(8,128)(2,1)S(1)} %get-tuple-element.62.query, ...), custom_call_target="tpu_custom_call" | custom-call | flops 3000000000 | bytes 16777216 | tf_op jit(solution)/shard_map/attend_1/pallas_call | solution.py:346
  39.0 1.1 %collective-permute-start.10 = (bf16[4,304,128]{2,1,0:T(8,128)(2,1)S(1)}, bf16[4,304,128]{2,1,0:T(8,128)(2,1)S(1)}, u32[]{:S(2)}, u32[]{:S(2)}) collective-permute-start(bf16[4,304,128]{2,1,0:T(8,128)(2,1)S(1)} %get-tuple-element.89), channel_id=1, source_target_pairs={{0,1},{1,0},{2,3},{3,2},{4,5},{5,4},{6,7},{7,6},{8,9},{9,8},{10,11... | collective-permute-start | bytes 933896 | tf_op jit(solution)/shard_map/ppermute | solution.py:438
  40.1 1.4 %collective-permute-start.8 = (bf16[4,304,128]{2,1,0:T(8,128)(2,1)S(1)}, bf16[4,304,128]{2,1,0:T(8,128)(2,1)S(1)}, u32[]{:S(2)}, u32[]{:S(2)}) collective-permute-start(bf16[4,304,128]{2,1,0:T(8,128)(2,1)S(1)} %get-tuple-element.84), channel_id=1, source_target_pairs={{0,4},{1,5},{2,6},{3,7},{4,0},{5,1},{6,2},{7,3},{8,12},{9,13},{10,... | collective-permute-start | bytes 933896 | tf_op jit(solution)/shard_map/ppermute | solution.py:438
  41.5 0.6 collective-permute-done.5.refs_1_
  42.2 2.5 %collective-permute-start.6 = (bf16[4,288,128]{2,1,0:T(8,128)(2,1)S(1)}, bf16[4,288,128]{2,1,0:T(8,128)(2,1)S(1)}, u32[]{:S(2)}, u32[]{:S(2)}) collective-permute-start(bf16[4,288,128]{2,1,0:T(8,128)(2,1)S(1)} %get-tuple-element.79), channel_id=1, source_target_pairs={{0,3},{1,2},{2,1},{3,0},{4,7},{5,6},{6,5},{7,4},{8,11},{9,10},{10,... | collective-permute-start | bytes 884744 | tf_op jit(solution)/shard_map/ppermute | solution.py:438
  44.7 2.9 %rest.1 = (bf16[4,688,128]{2,1,0:T(8,128)(2,1)S(1)}, bf16[4,688,128]{2,1,0:T(8,128)(2,1)S(1)}, bf16[4,672,128]{2,1,0:T(8,128)(2,1)S(1)}) custom-call(bf16[144,1024]{1,0:T(8,128)(2,1)S(1)} %get-tuple-element.67.first, bf16[112,1024]{1,0:T(8,128)(2,1)S(1)} %get-tuple-element.74.second, bf16[8,1024,1024]{2,1,0:T(8,128)(2,1)S(1)} %get-tuple-element.66.refs_3_.weight), custom_call_target="tpu_custom_call" | custom-call | flops 2100000000 | bytes 4194304 | tf_op jit(solution)/shard_map/rest/pallas_call | solution.py:229
  47.6 0.2 fold_4.3
  47.8 1.0 %collective-permute-start.13 = (bf16[2,688,128]{2,1,0:T(8,128)(2,1)S(1)}, bf16[2,688,128]{2,1,0:T(8,128)(2,1)S(1)}, u32[]{:S(2)}, u32[]{:S(2)}) collective-permute-start(bf16[2,688,128]{2,1,0:T(8,128)(2,1)S(1)} %get-tuple-element.93), channel_id=1, source_target_pairs={{0,4},{1,5},{2,6},{3,7},{4,0},{5,1},{6,2},{7,3},{8,12},{9,13},{10,... | collective-permute-start | bytes 1056776 | tf_op jit(solution)/shard_map/ppermute | solution.py:438
  48.8 0.2 fold_4.4
  49.0 3.7 %collective-permute-start.12 = (bf16[2,688,128]{2,1,0:T(8,128)(2,1)S(1)}, bf16[2,688,128]{2,1,0:T(8,128)(2,1)S(1)}, u32[]{:S(2)}, u32[]{:S(2)}) collective-permute-start(bf16[2,688,128]{2,1,0:T(8,128)(2,1)S(1)} %get-tuple-element.97), channel_id=1, source_target_pairs={{0,3},{1,2},{2,1},{3,0},{4,7},{5,6},{6,5},{7,4},{8,11},{9,10},{10,... | collective-permute-start | bytes 1056776 | tf_op jit(solution)/shard_map/ppermute | solution.py:438
  52.7 0.2 fold_4.5
  52.9 0.1 collective-permute-start.11
  53.0 3.5 %collective-permute-done.13.refs_1_ = bf16[2,688,128]{2,1,0:T(8,128)(2,1)S(1)} collective-permute-done((bf16[2,688,128]{2,1,0:T(8,128)(2,1)S(1)}, bf16[2,688,128]{2,1,0:T(8,128)(2,1)S(1)}, u32[]{:S(2)}, u32[]{:S(2)}) %collective-permute-start.13) | collective-permute-done | bytes 352288 | tf_op jit(solution)/shard_map/ppermute | solution.py:438
  56.5 2.7 %collective-permute-done.12.refs_1_ = bf16[2,688,128]{2,1,0:T(8,128)(2,1)S(1)} collective-permute-done((bf16[2,688,128]{2,1,0:T(8,128)(2,1)S(1)}, bf16[2,688,128]{2,1,0:T(8,128)(2,1)S(1)}, u32[]{:S(2)}, u32[]{:S(2)}) %collective-permute-start.12) | collective-permute-done | bytes 352288 | tf_op jit(solution)/shard_map/ppermute | solution.py:438
  59.4 3.0 %collective-permute-start.15 = (bf16[1,688,128]{2,1,0:T(8,128)(2,1)S(1)}, bf16[1,688,128]{2,1,0:T(8,128)(2,1)S(1)}, u32[]{:S(2)}, u32[]{:S(2)}) collective-permute-start(bf16[1,688,128]{2,1,0:T(8,128)(2,1)S(1)} %get-tuple-element.107), channel_id=1, source_target_pairs={{0,3},{1,2},{2,1},{3,0},{4,7},{5,6},{6,5},{7,4},{8,11},{9,10},{10,... | collective-permute-start | bytes 528392 | tf_op jit(solution)/shard_map/ppermute | solution.py:438
  62.5 0.6 collective-permute-start.14
  63.1 1.7 %collective-permute-done.16.refs_3_ = bf16[1,688,128]{2,1,0:T(8,128)(2,1)S(1)} collective-permute-done((bf16[1,688,128]{2,1,0:T(8,128)(2,1)S(1)}, bf16[1,688,128]{2,1,0:T(8,128)(2,1)S(1)}, u32[]{:S(2)}, u32[]{:S(2)}) %collective-permute-start.16) | collective-permute-done | bytes 176160 | tf_op jit(solution)/shard_map/ppermute | solution.py:438
  64.8 1.3 %collective-permute-done.15.refs_1_ = bf16[1,688,128]{2,1,0:T(8,128)(2,1)S(1)} collective-permute-done((bf16[1,688,128]{2,1,0:T(8,128)(2,1)S(1)}, bf16[1,688,128]{2,1,0:T(8,128)(2,1)S(1)}, u32[]{:S(2)}, u32[]{:S(2)}) %collective-permute-start.15) | collective-permute-done | bytes 176160 | tf_op jit(solution)/shard_map/ppermute | solution.py:438
  66.1 0.8 %finish_0.1.refs_2_ = bf16[256,1024]{1,0:T(8,128)(2,1)} custom-call(bf16[1,688,128]{2,1,0:T(8,128)(2,1)S(1)} %get-tuple-element.115.refs_0_, bf16[1,688,128]{2,1,0:T(8,128)(2,1)S(1)} %collective-permute-done.15.refs_1_, bf16[1,688,128]{2,1,0:T(8,128)(2,1)S(1)} %get-tuple-element.116.refs_2_, bf16[1,688,128]{2,1,0:T(8,128)(2,1)S(1)} %collective-permute-done.16.refs_3_), custom_call_target="tpu_custom_call" | custom-call | flops 300000 | bytes 1048576 | tf_op jit(solution)/shard_map/finish_0/pallas_call | solution.py:424
  66.9 1.1 %collective-permute-done.14.refs_1_ = bf16[1,672,128]{2,1,0:T(8,128)(2,1)S(1)} collective-permute-done((bf16[1,672,128]{2,1,0:T(8,128)(2,1)S(1)}, bf16[1,672,128]{2,1,0:T(8,128)(2,1)S(1)}, u32[]{:S(2)}, u32[]{:S(2)}) %collective-permute-start.14) | collective-permute-done | bytes 172064 | tf_op jit(solution)/shard_map/ppermute | solution.py:438
  68.0 0.7 %finish_2.1 = bf16[256,1024]{1,0:T(8,128)(2,1)} custom-call(bf16[1,672,128]{2,1,0:T(8,128)(2,1)S(1)} %get-tuple-element.113.refs_0_, bf16[1,672,128]{2,1,0:T(8,128)(2,1)S(1)} %collective-permute-done.14.refs_1_, bf16[256,1024]{1,0:T(8,128)(2,1)} %finish_0.1.refs_2_), custom_call_target="tpu_custom_call", output_to_operand_aliasing={{}: (2, {})} | custom-call | flops 300000 | bytes 1048576 | tf_op jit(solution)/shard_map/finish_2/pallas_call | solution.py:424
  (20 shorter events, 0.6 us)
Async XLA Ops:
  0.9 16.1 %collective-permute-start.3 = (bf16[2,256,128]{2,1,0:T(8,128)(2,1)S(1)}, bf16[2,256,128]{2,1,0:T(8,128)(2,1)S(1)}, u32[]{:S(2)}, u32[]{:S(2)}) collective-permute-start(bf16[2,256,128]{2,1,0:T(8,128)(2,1)S(1)} %pack.1), channel_id=1, source_target_pairs={{0,64},{8,72},{16,80},{24,88},{32,96},{40,104},{48,112},{56,120},{... | collective-permute-start | bytes 393224 | tf_op jit(solution)/shard_map/ppermute | solution.py:450
  2.4 14.6 %collective-permute-start.2 = (bf16[2,256,128]{2,1,0:T(8,128)(2,1)S(1)}, bf16[2,256,128]{2,1,0:T(8,128)(2,1)S(1)}, u32[]{:S(2)}, u32[]{:S(2)}) collective-permute-start(bf16[2,256,128]{2,1,0:T(8,128)(2,1)S(1)} %pack.1), channel_id=1, source_target_pairs={{0,48},{8,56},{16,64},{24,72},{32,80},{40,88},{48,96},{56,104},{64... | collective-permute-start | bytes 393224 | tf_op jit(solution)/shard_map/ppermute | solution.py:450
  7.1 9.8 %collective-permute-start.1 = (bf16[2,256,128]{2,1,0:T(8,128)(2,1)S(1)}, bf16[2,256,128]{2,1,0:T(8,128)(2,1)S(1)}, u32[]{:S(2)}, u32[]{:S(2)}) collective-permute-start(bf16[2,256,128]{2,1,0:T(8,128)(2,1)S(1)} %pack.1), channel_id=1, source_target_pairs={{0,32},{8,40},{16,48},{24,56},{32,64},{40,72},{48,80},{56,88},{64,... | collective-permute-start | bytes 393224 | tf_op jit(solution)/shard_map/ppermute | solution.py:450
  7.7 9.2 %collective-permute-start = (bf16[2,256,128]{2,1,0:T(8,128)(2,1)S(1)}, bf16[2,256,128]{2,1,0:T(8,128)(2,1)S(1)}, u32[]{:S(2)}, u32[]{:S(2)}) collective-permute-start(bf16[2,256,128]{2,1,0:T(8,128)(2,1)S(1)} %pack.1), channel_id=1, source_target_pairs={{0,16},{8,24},{16,32},{24,40},{32,48},{40,56},{48,64},{56,72},{64,... | collective-permute-start | bytes 393224 | tf_op jit(solution)/shard_map/ppermute | solution.py:450
  17.1 2.2 %collective-permute-start.4 = (bf16[5,2,256,128]{3,2,1,0:T(8,128)(2,1)S(1)}, bf16[5,2,256,128]{3,2,1,0:T(8,128)(2,1)S(1)}, u32[]{:S(2)}, u32[]{:S(2)}) collective-permute-start(bf16[5,2,256,128]{3,2,1,0:T(8,128)(2,1)S(1)} %bitcast_dynamic-update-slice_fusion.refs_0_), channel_id=1, source_target_pairs={{0,8},{8,0},{16,24},{24,16},{32,40},{40,32},{48,56},{56,48},{64,72... | collective-permute-start | bytes 1966088 | tf_op jit(solution)/shard_map/ppermute | solution.py:456
  26.7 12.3 %collective-permute-start.9 = (bf16[4,384,128]{2,1,0:T(8,128)(2,1)S(1)}, bf16[4,384,128]{2,1,0:T(8,128)(2,1)S(1)}, u32[]{:S(2)}, u32[]{:S(2)}) collective-permute-start(bf16[4,384,128]{2,1,0:T(8,128)(2,1)S(1)} %get-tuple-element.87), channel_id=1, source_target_pairs={{0,1},{1,0},{2,3},{3,2},{4,5},{5,4},{6,7},{7,6},{8,9},{9,8},{10,11... | collective-permute-start | bytes 1179656 | tf_op jit(solution)/shard_map/ppermute | solution.py:438
  28.8 11.3 %collective-permute-start.7 = (bf16[4,384,128]{2,1,0:T(8,128)(2,1)S(1)}, bf16[4,384,128]{2,1,0:T(8,128)(2,1)S(1)}, u32[]{:S(2)}, u32[]{:S(2)}) collective-permute-start(bf16[4,384,128]{2,1,0:T(8,128)(2,1)S(1)} %get-tuple-element.82), channel_id=1, source_target_pairs={{0,4},{1,5},{2,6},{3,7},{4,0},{5,1},{6,2},{7,3},{8,12},{9,13},{10,... | collective-permute-start | bytes 1179656 | tf_op jit(solution)/shard_map/ppermute | solution.py:438
  30.3 11.8 %collective-permute-start.5 = (bf16[4,384,128]{2,1,0:T(8,128)(2,1)S(1)}, bf16[4,384,128]{2,1,0:T(8,128)(2,1)S(1)}, u32[]{:S(2)}, u32[]{:S(2)}) collective-permute-start(bf16[4,384,128]{2,1,0:T(8,128)(2,1)S(1)} %get-tuple-element.77), channel_id=1, source_target_pairs={{0,3},{1,2},{2,1},{3,0},{4,7},{5,6},{6,5},{7,4},{8,11},{9,10},{10,... | collective-permute-start | bytes 1179656 | tf_op jit(solution)/shard_map/ppermute | solution.py:438
  39.0 8.7 %collective-permute-start.10 = (bf16[4,304,128]{2,1,0:T(8,128)(2,1)S(1)}, bf16[4,304,128]{2,1,0:T(8,128)(2,1)S(1)}, u32[]{:S(2)}, u32[]{:S(2)}) collective-permute-start(bf16[4,304,128]{2,1,0:T(8,128)(2,1)S(1)} %get-tuple-element.89), channel_id=1, source_target_pairs={{0,1},{1,0},{2,3},{3,2},{4,5},{5,4},{6,7},{7,6},{8,9},{9,8},{10,11... | collective-permute-start | bytes 933896 | tf_op jit(solution)/shard_map/ppermute | solution.py:438
  40.1 8.7 %collective-permute-start.8 = (bf16[4,304,128]{2,1,0:T(8,128)(2,1)S(1)}, bf16[4,304,128]{2,1,0:T(8,128)(2,1)S(1)}, u32[]{:S(2)}, u32[]{:S(2)}) collective-permute-start(bf16[4,304,128]{2,1,0:T(8,128)(2,1)S(1)} %get-tuple-element.84), channel_id=1, source_target_pairs={{0,4},{1,5},{2,6},{3,7},{4,0},{5,1},{6,2},{7,3},{8,12},{9,13},{10,... | collective-permute-start | bytes 933896 | tf_op jit(solution)/shard_map/ppermute | solution.py:438
  42.2 10.6 %collective-permute-start.6 = (bf16[4,288,128]{2,1,0:T(8,128)(2,1)S(1)}, bf16[4,288,128]{2,1,0:T(8,128)(2,1)S(1)}, u32[]{:S(2)}, u32[]{:S(2)}) collective-permute-start(bf16[4,288,128]{2,1,0:T(8,128)(2,1)S(1)} %get-tuple-element.79), channel_id=1, source_target_pairs={{0,3},{1,2},{2,1},{3,0},{4,7},{5,6},{6,5},{7,4},{8,11},{9,10},{10,... | collective-permute-start | bytes 884744 | tf_op jit(solution)/shard_map/ppermute | solution.py:438
  47.8 8.6 %collective-permute-start.13 = (bf16[2,688,128]{2,1,0:T(8,128)(2,1)S(1)}, bf16[2,688,128]{2,1,0:T(8,128)(2,1)S(1)}, u32[]{:S(2)}, u32[]{:S(2)}) collective-permute-start(bf16[2,688,128]{2,1,0:T(8,128)(2,1)S(1)} %get-tuple-element.93), channel_id=1, source_target_pairs={{0,4},{1,5},{2,6},{3,7},{4,0},{5,1},{6,2},{7,3},{8,12},{9,13},{10,... | collective-permute-start | bytes 1056776 | tf_op jit(solution)/shard_map/ppermute | solution.py:438
  49.0 10.2 %collective-permute-start.12 = (bf16[2,688,128]{2,1,0:T(8,128)(2,1)S(1)}, bf16[2,688,128]{2,1,0:T(8,128)(2,1)S(1)}, u32[]{:S(2)}, u32[]{:S(2)}) collective-permute-start(bf16[2,688,128]{2,1,0:T(8,128)(2,1)S(1)} %get-tuple-element.97), channel_id=1, source_target_pairs={{0,3},{1,2},{2,1},{3,0},{4,7},{5,6},{6,5},{7,4},{8,11},{9,10},{10,... | collective-permute-start | bytes 1056776 | tf_op jit(solution)/shard_map/ppermute | solution.py:438
  52.9 9.5 %collective-permute-start.11 = (bf16[2,672,128]{2,1,0:T(8,128)(2,1)S(1)}, bf16[2,672,128]{2,1,0:T(8,128)(2,1)S(1)}, u32[]{:S(2)}, u32[]{:S(2)}) collective-permute-start(bf16[2,672,128]{2,1,0:T(8,128)(2,1)S(1)} %get-tuple-element.102), channel_id=1, source_target_pairs={{0,1},{1,0},{2,3},{3,2},{4,5},{5,4},{6,7},{7,6},{8,9},{9,8},{10,11... | collective-permute-start | bytes 1032200 | tf_op jit(solution)/shard_map/ppermute | solution.py:438
  59.3 5.5 %collective-permute-start.16 = (bf16[1,688,128]{2,1,0:T(8,128)(2,1)S(1)}, bf16[1,688,128]{2,1,0:T(8,128)(2,1)S(1)}, u32[]{:S(2)}, u32[]{:S(2)}) collective-permute-start(bf16[1,688,128]{2,1,0:T(8,128)(2,1)S(1)} %get-tuple-element.110), channel_id=1, source_target_pairs={{0,1},{1,0},{2,3},{3,2},{4,5},{5,4},{6,7},{7,6},{8,9},{9,8},{10,11... | collective-permute-start | bytes 528392 | tf_op jit(solution)/shard_map/ppermute | solution.py:438
  59.4 6.7 %collective-permute-start.15 = (bf16[1,688,128]{2,1,0:T(8,128)(2,1)S(1)}, bf16[1,688,128]{2,1,0:T(8,128)(2,1)S(1)}, u32[]{:S(2)}, u32[]{:S(2)}) collective-permute-start(bf16[1,688,128]{2,1,0:T(8,128)(2,1)S(1)} %get-tuple-element.107), channel_id=1, source_target_pairs={{0,3},{1,2},{2,1},{3,0},{4,7},{5,6},{6,5},{7,4},{8,11},{9,10},{10,... | collective-permute-start | bytes 528392 | tf_op jit(solution)/shard_map/ppermute | solution.py:438
  62.5 5.5 %collective-permute-start.14 = (bf16[1,672,128]{2,1,0:T(8,128)(2,1)S(1)}, bf16[1,672,128]{2,1,0:T(8,128)(2,1)S(1)}, u32[]{:S(2)}, u32[]{:S(2)}) collective-permute-start(bf16[1,672,128]{2,1,0:T(8,128)(2,1)S(1)} %get-tuple-element.114), channel_id=1, source_target_pairs={{0,4},{1,5},{2,6},{3,7},{4,0},{5,1},{6,2},{7,3},{8,12},{9,13},{10,... | collective-permute-start | bytes 516104 | tf_op jit(solution)/shard_map/ppermute | solution.py:438
